TPU v7x, 512 devices: a whole 4x8x8 slice. The times are simulated.
512 devices in a mesh: row: 16 (over x, z_hi, core), col: 32 (over y, z_lo).
Axes of the slice: x: 4, y: 8, z: 8 (z_hi: 2, z_lo: 4; z = z_hi * 4 + z_lo), core: 2. Of those that a mesh axis runs over, the one named last changes fastest.
Arguments:
- first_alignment_matrix: float32 [64, 512, 32], P('row', 'col'), may hold values from -6 to 6
- second_alignment_matrix: float32 [64, 512, 32], P('row', 'col'), may hold values from -6 to 6
- couple_delta_sensitivity: float32 [512, 512, 128], P('row', 'col'), may hold values from -6 to 6
- mapping_matrix: float32 [1024, 128], replicated, may hold values from -0.1875 to 0.1875
Outputs:
- grad_left: float32 [64, 512, 32], P('row', 'col')
- grad_right: float32 [64, 512, 32], P('row', 'col')
All inputs are finite; a program needn't handle non-finite values.
Results may differ from a plain program's by a relative error of at most 0.0003.
Values sent between devices are 32-bit elements; how exact they have to be, the bound alone decides.
No kernel may reach another device: no remote copies, remote signals or barrier semaphores. Data moves between devices by JAX's collectives and lax.ppermute only.
A program may use at most 64 MiB of HBM per device.

v0:
```python
import jax
import jax.numpy as jnp
from jax import lax
from jax.sharding import PartitionSpec as P


def on_device(
    first_alignment_matrix, second_alignment_matrix, couple_delta_sensitivity, mapping_matrix
):
    exact_arithmetic = lax.Precision.HIGHEST
    sequences_on_device = first_alignment_matrix.shape[0]
    row_count = lax.axis_size("row")
    summed_extent = sequences_on_device * row_count
    first_feature_number = first_alignment_matrix.shape[2]
    second_feature_number = second_alignment_matrix.shape[2]
    pair_chans = couple_delta_sensitivity.shape[2]
    tile_i = couple_delta_sensitivity.shape[0]
    tile_j = couple_delta_sensitivity.shape[1]
    second_collected = lax.all_gather(second_alignment_matrix, "row", axis=0, tiled=True)
    second_flat = second_collected.reshape(summed_extent, tile_j * second_feature_number)
    expanded_outer_term = lax.all_gather(first_alignment_matrix, "col", axis=1, tiled=True)
    left_all = lax.all_to_all(expanded_outer_term, "row", split_axis=1, concat_axis=0, tiled=True)
    weight3 = mapping_matrix.reshape(first_feature_number, second_feature_number, pair_chans)
    block_rows = tile_i // 4
    grad_blocks = couple_delta_sensitivity.reshape(4, block_rows, tile_j, pair_chans)
    left_blocks = jnp.transpose(
        left_all.reshape(summed_extent, 4, block_rows, first_feature_number), (1, 0, 2, 3)
    )
    left_blocks = left_blocks.reshape(4, summed_extent, block_rows * first_feature_number)

    def step(carry, pieces):
        grad_tile, left_tile = pieces
        outer_matrix = jnp.einsum("ijp,cep->icje", grad_tile, weight3, precision=exact_arithmetic)
        outer_matrix = outer_matrix.reshape(
            block_rows * first_feature_number, tile_j * second_feature_number
        )
        left_part = (
            jnp.einsum("sk,xk->sx", second_flat, outer_matrix, precision=exact_arithmetic)
            / summed_extent
        )
        carry = (
            carry
            + jnp.einsum("sx,xk->sk", left_tile, outer_matrix, precision=exact_arithmetic)
            / summed_extent
        )
        return (carry, left_part.reshape(summed_extent, block_rows, first_feature_number))

    start_right = jnp.zeros((summed_extent, tile_j * second_feature_number), jnp.float32)
    right_flat, left_parts = lax.scan(step, start_right, (grad_blocks, left_blocks))
    right_part = right_flat.reshape(summed_extent, tile_j, second_feature_number)
    left_part = jnp.transpose(left_parts, (1, 0, 2, 3)).reshape(
        summed_extent, tile_i, first_feature_number
    )
    moved = lax.all_to_all(left_part, "row", split_axis=0, concat_axis=1, tiled=True)
    grad_left = lax.psum_scatter(moved, "col", scatter_dimension=1, tiled=True)
    grad_right = lax.psum_scatter(right_part, "row", scatter_dimension=0, tiled=True)
    return (grad_left, grad_right)


def solution(mesh):
    return jax.shard_map(
        on_device,
        mesh=mesh,
        in_specs=(P("row", "col", None), P("row", "col", None), P("row", "col", None), P()),
        out_specs=(P("row", "col", None), P("row", "col", None)),
        check_vma=False,
    )
```

profile of v0, /device:TPU:2, one launch (start us, length us, event | category | flops | bytes accessed | tf_op | source)
XLA Modules:
  0.0 511.3 jit_solution(5669458877101053021)
XLA Ops:
  8.0 0.8 copy.40
  8.8 88.3 %all_gather.6 = f32[4,512,32]{2,0,1:T(4,128)S(1)} all-gather(f32[4,16,32]{2,0,1:T(4,128)S(1)} %copy.40), channel_id=1, replica_groups=mesh['row'=16,'col'=32] {'col'}, dimensions={1}, use_global_device_ids=true | all-gather | bytes 270336 | tf_op jit(solution)/shard_map/all_gather | solution.py:21
  97.1 1.4 reshape.42
  98.4 10.1 %all-to-all-start = ((f32[16,1,4096]{2,1,0:T(1,128)}), f32[16,1,4096]{2,1,0:T(1,128)S(1)}, u32[]{:S(2)}, u32[]{:S(2)}) async-start(f32[16,1,4096]{2,1,0:T(1,128)} %reshape.42), calls=%async_computation | async-start | bytes 524288 | tf_op jit(solution)/shard_map/all_to_all | solution.py:22
  108.6 30.9 %all_gather.7 = f32[64,16,32]{2,1,0:T(8,128)S(1)} all-gather(f32[4,16,32]{2,1,0:T(8,128)S(1)} %copy-done.1), channel_id=1, replica_groups=mesh['row'=16,'col'=32] {'row'}, dimensions={0}, use_global_device_ids=true | all-gather | bytes 139264 | tf_op jit(solution)/shard_map/all_gather | solution.py:19
  140.4 1.3 reduce
  142.9 0.9 copy.44
  143.8 27.5 %while.13 = (s32[]{:T(128)}, f32[64,512]{1,0:T(8,128)S(1)}, f32[4,64,8,32]{1,3,2,0:T(8,128)}, f32[4,64,256]{2,1,0:T(8,128)}, f32[4,8,16,128]{3,2,1,0:T(8,128)}, ...) while((s32[]{:T(128)}, f32[64,512]{1,0:T(8,128)S(1)}, ...), condition=%wide.region_1.2_spmd.clone, body=%wide.region_0.1_spmd.clone.sunk | while | flops 402767872 | bytes 4064871 | solution.py:49
  143.8 3.4 convolution_bitcast_fusion.2
  147.2 0.8 reshape.47
  148.0 1.3 fusion.26
  150.0 0.7 constant_dynamic-update-slice_fusion.2
  150.7 3.4 convolution_bitcast_fusion.2
  154.1 0.8 reshape.47
  154.9 1.3 fusion.26
  156.9 0.7 constant_dynamic-update-slice_fusion.2
  157.5 3.4 convolution_bitcast_fusion.2
  160.9 0.8 reshape.47
  161.8 1.3 fusion.26
  163.7 0.7 constant_dynamic-update-slice_fusion.2
  164.4 3.4 convolution_bitcast_fusion.2
  167.8 0.8 reshape.47
  168.6 1.3 fusion.26
  170.6 0.7 constant_dynamic-update-slice_fusion.2
  171.3 2.0 copy.46
  173.7 15.7 %all_to_all.33 = f32[16,1,4096]{2,1,0:T(1,128)S(1)} all-to-all(f32[16,1,4096]{2,1,0:T(1,128)S(1)} %reshape.44), channel_id=1, replica_groups=mesh['row'=16,'col'=32] {'row'}, dimensions={0} | all-to-all | bytes 524288 | tf_op jit(solution)/shard_map/all_to_all | solution.py:54
  189.4 1.3 reduce.1
  191.0 1.7 copy.53
  193.0 1.1 copy.50
  194.0 1.3 dynamic-slice
  196.0 306.5 %all-reduce.3.cloned.1.call-done = f32[4,512,32]{2,0,1:T(4,128)} async-done(((f32[4,512,32]{2,0,1:T(4,128)}), f32[4,512,32]{2,0,1:T(4,128)}) %all-reduce.3.cloned.1.call-update) | async-done | bytes 262160
  502.5 0.8 constant_dynamic-slice_fusion
  (30 shorter events, 6.6 us)
Async XLA Ops:
  8.0 100.6 %copy-start.1 = (f32[4,16,32]{2,1,0:T(8,128)S(1)}, f32[4,16,32]{2,1,0:T(8,128)}, u32[]{:S(2)}) copy-start(f32[4,16,32]{2,1,0:T(8,128)} %param.7) | copy-start | bytes 24580
  98.4 41.4 %all-to-all-start = ((f32[16,1,4096]{2,1,0:T(1,128)}), f32[16,1,4096]{2,1,0:T(1,128)S(1)}, u32[]{:S(2)}, u32[]{:S(2)}) async-start(f32[16,1,4096]{2,1,0:T(1,128)} %reshape.42), calls=%async_computation | async-start | bytes 524288 | tf_op jit(solution)/shard_map/all_to_all | solution.py:22
  108.5 394.0 %all-reduce.3.cloned.1.call-start = ((), (), s32[]{:S(2)}) async-start(), calls=%async_computation.4 | async-start | bytes 2097152
  142.2 1.6 copy-start
  192.8 311.1 %reduce-scatter.2.cloned.1.call-start = ((), (), s32[]{:S(2)}) async-start(), calls=%async_computation.3 | async-start | bytes 557056 | tf_op jit(solution)/shard_map/reduce_scatter | solution.py:56
Sparse Core Ops, SparseCore 0:
  192.9 309.5 all-reduce.2
Sparse Core Ops, SparseCore 1:
  198.5 81.8 reduce-scatter.1
where the time goes:
time: 512 us; the launch traced here: 511 us
  waiting for transfers between devices  307 us (60%)
  blocking collectives  135 us (26%)
  matrix products  21 us (4%)
  local copies, waits for them, and re-layouts  19.8 us (4%)
  between operations  16.3 us (3%)
  starting transfers between devices  10.1 us (2%)
    unnamed x3, waiting for transfers between devices  307 us
    all_gather x1, blocking collectives, on_device(): lax.all_gather(first_alignment_matrix, 'col', axis=1, tiled=True)  88.3 us
    all_gather x1, blocking collectives, on_device(): lax.all_gather(second_alignment_matrix, 'row', axis=0, tiled=True)  30.9 us
    all_to_all x1, blocking collectives, on_device(): lax.all_to_all(left_part, 'row', split_axis=0, concat_axis=1, tiled=True)  15.7 us
    dot_general x4, matrix products, step(): jnp.einsum('ijp,cep->icje', grad_tile, weight3, precision=exact_arithmetic)  13.5 us
  transfers between devices with their start and end apart: 3, of which 1 were waited for; matrix products, arithmetic and copies ran while one was open for 1% of the time, Pallas kernels for 0%

commit v1 on v0

v1 whole, which is shorter than its diff:
```python
import jax
import jax.numpy as jnp
from jax import lax
from jax.sharding import PartitionSpec as P

LANES = 128


def swap_pairs(rows, cols):
    half = cols // rows
    return [
        (r * cols + c, (c // half) * cols + half * r + c % half)
        for r in range(rows)
        for c in range(cols)
    ]


def to_all(block, axis):
    count = lax.axis_size(axis)
    spread = jnp.broadcast_to(block[None], (count,) + block.shape)
    return lax.all_to_all(spread, axis, split_axis=0, concat_axis=0, tiled=True)


def sum_to_owner(chunks, axis):
    moved = lax.all_to_all(chunks, axis, split_axis=0, concat_axis=0, tiled=True)
    return moved.sum(axis=0)


def on_device(left, right, grad, mapping):
    exact = lax.Precision.HIGH
    rows, cols = lax.axis_size("row"), lax.axis_size("col")
    half = cols // rows
    seqs, res, feat_c = left.shape
    feat_e = right.shape[2]
    tile_i, tile_j, pair = grad.shape
    total = seqs * rows
    pairs = swap_pairs(rows, cols)

    left_moved = lax.ppermute(left.reshape(-1, LANES), ("row", "col"), pairs)
    right_all = to_all(right.reshape(-1, LANES), "row")
    left_all = to_all(left_moved, "col")
    right_flat = right_all.reshape(total, tile_j * feat_e)
    left_flat = left_all.reshape(rows, half, seqs, res, feat_c).transpose(0, 2, 1, 3, 4)
    left_flat = left_flat.reshape(total, tile_i * feat_c)

    weight3 = mapping.reshape(feat_c, feat_e, pair)
    outer = jnp.einsum("ijp,cep->icje", grad, weight3, precision=exact)
    outer = outer.reshape(tile_i * feat_c, tile_j * feat_e)
    left_part = jnp.einsum("sk,xk->sx", right_flat, outer, precision=exact) / total
    right_part = jnp.einsum("sx,xk->sk", left_flat, outer, precision=exact) / total

    chunks = left_part.reshape(rows, seqs, half, res, feat_c).transpose(0, 2, 1, 3, 4)
    left_sum = sum_to_owner(chunks.reshape(cols, -1, LANES), "col")
    grad_left = lax.ppermute(left_sum, ("row", "col"), pairs).reshape(left.shape)
    grad_right = sum_to_owner(right_part.reshape(rows, -1, LANES), "row").reshape(right.shape)
    return (grad_left, grad_right)


def solution(mesh):
    spec = P("row", "col", None)
    return jax.shard_map(
        on_device,
        mesh=mesh,
        in_specs=(spec, spec, spec, P()),
        out_specs=(spec, spec),
        check_vma=False,
    )
```

time: 512 us -> 118 us (0.23)
  the two profiles are of different devices: /device:TPU:2 before, /device:TPU:12 now
where the time goes in v1:
time: 118 us; the launch traced here: 117 us
  starting transfers between devices  58.2 us (49%)
  local copies, waits for them, and re-layouts  31.7 us (27%)
  waiting for transfers between devices  18.2 us (15%)
  matrix products  8.48 us (7%)
    all_to_all x2, starting transfers between devices, sum_to_owner(): lax.all_to_all(chunks, axis, split_axis=0, concat_axis=0, tiled=True)  21.5 us
    all_to_all x2, starting transfers between devices, to_all(): return lax.all_to_all(spread, axis, split_axis=0, concat_axis=0, tiled=True)  17.6 us
    ppermute x1, starting transfers between devices, on_device(): left_moved = lax.ppermute(left.reshape(-1, LANES), ('row', 'col'), pairs)  11.5 us
    transpose x1, local copies, waits for them, and re-layouts, on_device(): outer = jnp.einsum('ijp,cep->icje', grad, weight3, precision=exact)  9.03 us
    ppermute x1, starting transfers between devices, on_device(): lax.ppermute(left_sum, ('row', 'col'), pairs).reshape(left.shape)  7.53 us
    ppermute x1, waiting for transfers between devices, on_device(): lax.ppermute(left_sum, ('row', 'col'), pairs).reshape(left.shape)  7.07 us
    all_to_all x2, waiting for transfers between devices, sum_to_owner(): lax.all_to_all(chunks, axis, split_axis=0, concat_axis=0, tiled=True)  6.79 us
    dot_general x1, matrix products, on_device(): outer = jnp.einsum('ijp,cep->icje', grad, weight3, precision=exact)  6.67 us
  transfers between devices with their start and end apart: 6, of which 4 were waited for; matrix products, arithmetic and copies ran while one was open for 32% of the time, Pallas kernels for 0%

profile of v1, /device:TPU:12, one launch (start us, length us, event | category | flops | bytes accessed | tf_op | source)
XLA Modules:
  0.0 117.3 jit_solution(2720403094384883082)
XLA Ops:
  0.6 0.0 copy-start
  0.6 0.9 broadcast_in_dim.6
  1.5 0.7 broadcast_in_dim.14
  2.2 13.3 %all-to-all-start = ((f32[16,16,128]{2,1,0:T(8,128)}), f32[16,16,128]{2,1,0:T(8,128)S(1)}, u32[]{:S(2)}, u32[]{:S(2)}) async-start(f32[16,16,128]{2,1,0:T(8,128)} %broadcast_in_dim.14), calls=%async_computation | async-start | bytes 262144 | tf_op jit(solution)/shard_map/all_to_all | solution.py:21
  15.5 0.8 reshape.45
  16.3 11.5 %collective-permute-start.1 = (f32[16,128]{1,0:T(8,128)S(1)}, f32[16,128]{1,0:T(8,128)S(1)}, u32[]{:S(2)}, u32[]{:S(2)}) collective-permute-start(f32[16,128]{1,0:T(8,128)S(1)} %reshape.45), channel_id=1, source_target_pairs={{0,0},{1,1},{2,32},{3,33},{4,64},{5,65},{6,96},{7,97},{8,128},{9,1... | collective-permute-start | bytes 24584 | tf_op jit(solution)/shard_map/ppermute | solution.py:39
  27.8 4.3 %collective-permute-done.1 = f32[16,128]{1,0:T(8,128)S(1)} collective-permute-done((f32[16,128]{1,0:T(8,128)S(1)}, f32[16,128]{1,0:T(8,128)S(1)}, u32[]{:S(2)}, u32[]{:S(2)}) %collective-permute-start.1) | collective-permute-done | bytes 8224 | tf_op jit(solution)/shard_map/ppermute | solution.py:39
  32.1 0.0 all-to-all-done
  32.1 0.7 broadcast_in_dim.15
  32.8 4.3 %all-to-all-start.2 = ((f32[32,16,128]{2,1,0:T(8,128)}), f32[32,16,128]{2,1,0:T(8,128)S(1)}, u32[]{:S(2)}, u32[]{:S(2)}) async-start(f32[32,16,128]{2,1,0:T(8,128)} %broadcast_in_dim.15), calls=%async_computation.2 | async-start | bytes 524288 | tf_op jit(solution)/shard_map/all_to_all | solution.py:21
  37.1 0.0 copy-done
  37.1 6.7 %convolution_bitcast_fusion = f32[32,32,16,32]{0,3,2,1:T(8,128)} fusion(f32[32,32,128,1]{2,1,3,0:T(8,128)S(1)} %bitcast.29, f32[32,16,128]{2,1,0:T(8,128)} %param.6), kind=kOutput, calls=%fused_computation | convolution fusion | flops 402653184 | bytes 2883584 | tf_op jit(solution)/shard_map/ijp,cep->icje/dot_general | solution.py:47
  43.8 9.0 %copy.11 = f32[32,32,16,32]{3,2,1,0:T(8,128)} copy(f32[32,32,16,32]{0,3,2,1:T(8,128)} %convolution_bitcast_fusion) | data formatting | bytes 4194304 | tf_op jit(solution)/shard_map/ijp,cep->icje/transpose | solution.py:47
  52.8 6.2 %reshape.40 = f32[1024,512]{1,0:T(8,128)S(1)} reshape(f32[32,32,16,32]{3,2,1,0:T(8,128)} %copy.11) | data formatting | bytes 4194304 | tf_op jit(solution)/shard_map/reshape | solution.py:48
  59.1 1.1 fusion
  60.2 1.4 %reshape.42 = f32[16,4,2,16,32]{4,3,2,1,0:T(8,128)} reshape(f32[64,1024]{1,0:T(8,128)S(1)} %fusion) | data formatting | bytes 524288 | tf_op jit(solution)/shard_map/reshape | solution.py:52
  61.6 2.3 %copy.20 = f32[16,4,2,16,32]{4,3,1,2,0:T(8,128)} copy(f32[16,4,2,16,32]{4,3,2,1,0:T(8,128)} %reshape.42) | data formatting | bytes 524288 | tf_op jit(solution)/shard_map/reshape | solution.py:52
  63.9 2.2 %reshape.43 = f32[32,16,128]{2,1,0:T(8,128)} reshape(f32[16,2,4,16,32]{4,3,2,1,0:T(8,128)} %bitcast.30) | data formatting | bytes 524288 | tf_op jit(solution)/shard_map/reshape | solution.py:53
  66.1 0.0 all-to-all-done.2
  66.1 10.1 %all-to-all-start.1 = ((f32[32,16,128]{2,1,0:T(8,128)}), f32[32,16,128]{2,1,0:T(8,128)S(1)}, u32[]{:S(2)}, u32[]{:S(2)}) async-start(f32[32,16,128]{2,1,0:T(8,128)} %reshape.43), calls=%async_computation.1 | async-start | bytes 524288 | tf_op jit(solution)/shard_map/all_to_all | solution.py:25
  76.2 1.2 %reshape.46 = f32[16,2,4,16,32]{4,3,2,1,0:T(8,128)} reshape(f32[32,16,128]{2,1,0:T(8,128)S(1)} %all-to-all-done.2) | data formatting | bytes 524288 | tf_op jit(solution)/shard_map/reshape | solution.py:43
  77.5 2.4 %copy.13 = f32[16,4,2,16,32]{4,3,2,1,0:T(8,128)} copy(f32[16,4,2,16,32]{4,3,1,2,0:T(8,128)} %bitcast.31) | data formatting | bytes 524288 | tf_op jit(solution)/shard_map/transpose | solution.py:43
  79.8 1.7 %reshape.47 = f32[64,1024]{1,0:T(8,128)S(1)} reshape(f32[16,4,2,16,32]{4,3,2,1,0:T(8,128)} %copy.13) | data formatting | bytes 524288 | tf_op jit(solution)/shard_map/reshape | solution.py:44
  81.6 0.7 fusion.1
  82.3 0.7 reshape.48
  83.0 6.3 %all-to-all-done.1 = f32[32,16,128]{2,1,0:T(8,128)S(1)} async-done(((f32[32,16,128]{2,1,0:T(8,128)}), f32[32,16,128]{2,1,0:T(8,128)S(1)}, u32[]{:S(2)}, u32[]{:S(2)}) %all-to-all-start.1) | async-done | bytes 262176 | tf_op jit(solution)/shard_map/all_to_all | solution.py:25
  89.3 11.5 %all-to-all-start.3 = ((f32[16,16,128]{2,1,0:T(8,128)}), f32[16,16,128]{2,1,0:T(8,128)S(1)}, u32[]{:S(2)}, u32[]{:S(2)}) async-start(f32[16,16,128]{2,1,0:T(8,128)} %reshape.48), calls=%async_computation.3 | async-start | bytes 262144 | tf_op jit(solution)/shard_map/all_to_all | solution.py:25
  100.8 7.5 %collective-permute-start = (f32[16,128]{1,0:T(8,128)S(1)}, f32[16,128]{1,0:T(8,128)S(1)}, u32[]{:S(2)}, u32[]{:S(2)}) collective-permute-start(f32[16,128]{1,0:T(8,128)S(1)} %reduce_sum.18), channel_id=1, source_target_pairs={{0,0},{1,1},{2,32},{3,33},{4,64},{5,65},{6,96},{7,97},{8,128},{9,1... | collective-permute-start | bytes 24584 | tf_op jit(solution)/shard_map/ppermute | solution.py:54
  108.3 0.4 all-to-all-done.3
  108.8 0.7 reshape.49
  109.5 7.1 %collective-permute-done = f32[16,128]{1,0:T(8,128)S(1)} collective-permute-done((f32[16,128]{1,0:T(8,128)S(1)}, f32[16,128]{1,0:T(8,128)S(1)}, u32[]{:S(2)}, u32[]{:S(2)}) %collective-permute-start) | collective-permute-done | bytes 8224 | tf_op jit(solution)/shard_map/ppermute | solution.py:54
  116.6 0.7 reshape.44
  (3 shorter events, 0.1 us)
Async XLA Ops:
  0.6 36.5 %copy-start = (f32[1024,128]{1,0:T(8,128)S(1)}, f32[1024,128]{1,0:T(8,128)}, u32[]{:S(2)}) copy-start(f32[1024,128]{1,0:T(8,128)} %param.7) | copy-start | bytes 1572868
  2.2 29.9 %all-to-all-start = ((f32[16,16,128]{2,1,0:T(8,128)}), f32[16,16,128]{2,1,0:T(8,128)S(1)}, u32[]{:S(2)}, u32[]{:S(2)}) async-start(f32[16,16,128]{2,1,0:T(8,128)} %broadcast_in_dim.14), calls=%async_computation | async-start | bytes 262144 | tf_op jit(solution)/shard_map/all_to_all | solution.py:21
  16.3 15.8 %collective-permute-start.1 = (f32[16,128]{1,0:T(8,128)S(1)}, f32[16,128]{1,0:T(8,128)S(1)}, u32[]{:S(2)}, u32[]{:S(2)}) collective-permute-start(f32[16,128]{1,0:T(8,128)S(1)} %reshape.45), channel_id=1, source_target_pairs={{0,0},{1,1},{2,32},{3,33},{4,64},{5,65},{6,96},{7,97},{8,128},{9,1... | collective-permute-start | bytes 24584 | tf_op jit(solution)/shard_map/ppermute | solution.py:39
  32.8 33.3 %all-to-all-start.2 = ((f32[32,16,128]{2,1,0:T(8,128)}), f32[32,16,128]{2,1,0:T(8,128)S(1)}, u32[]{:S(2)}, u32[]{:S(2)}) async-start(f32[32,16,128]{2,1,0:T(8,128)} %broadcast_in_dim.15), calls=%async_computation.2 | async-start | bytes 524288 | tf_op jit(solution)/shard_map/all_to_all | solution.py:21
  66.1 23.2 %all-to-all-start.1 = ((f32[32,16,128]{2,1,0:T(8,128)}), f32[32,16,128]{2,1,0:T(8,128)S(1)}, u32[]{:S(2)}, u32[]{:S(2)}) async-start(f32[32,16,128]{2,1,0:T(8,128)} %reshape.43), calls=%async_computation.1 | async-start | bytes 524288 | tf_op jit(solution)/shard_map/all_to_all | solution.py:25
  89.3 19.5 %all-to-all-start.3 = ((f32[16,16,128]{2,1,0:T(8,128)}), f32[16,16,128]{2,1,0:T(8,128)S(1)}, u32[]{:S(2)}, u32[]{:S(2)}) async-start(f32[16,16,128]{2,1,0:T(8,128)} %reshape.48), calls=%async_computation.3 | async-start | bytes 262144 | tf_op jit(solution)/shard_map/all_to_all | solution.py:25
  100.8 15.8 %collective-permute-start = (f32[16,128]{1,0:T(8,128)S(1)}, f32[16,128]{1,0:T(8,128)S(1)}, u32[]{:S(2)}, u32[]{:S(2)}) collective-permute-start(f32[16,128]{1,0:T(8,128)S(1)} %reduce_sum.18), channel_id=1, source_target_pairs={{0,0},{1,1},{2,32},{3,33},{4,64},{5,65},{6,96},{7,97},{8,128},{9,1... | collective-permute-start | bytes 24584 | tf_op jit(solution)/shard_map/ppermute | solution.py:54

commit v2 on v1

v2 whole, which is shorter than its diff:
```python
import jax
import jax.numpy as jnp
from jax import lax
from jax.experimental import pallas as pl
from jax.experimental.pallas import tpu as pltpu
from jax.sharding import PartitionSpec as P

LANES = 128
NT = (((1,), (1,)), ((), ()))
NN = (((1,), (0,)), ((), ()))


def split(x):
    high = x.astype(jnp.bfloat16)
    return high, (x - high.astype(jnp.float32)).astype(jnp.bfloat16)


def product(a, b, dims):
    return lax.dot_general(a, b, dims, preferred_element_type=jnp.float32)


def swap_lane_groups(x, width):
    lane = lax.broadcasted_iota(jnp.int32, x[0].shape, 1)
    count, step = len(x), len(x) // 2
    while step:
        first = (lane // (width * step)) % 2 == 0
        y = list(x)
        for j in range(count):
            if (j // step) % 2 == 0:
                a, b, shift = x[j], x[j + step], width * step
                y[j] = jnp.where(first, a, pltpu.roll(b, shift, 1))
                y[j + step] = jnp.where(first, pltpu.roll(a, LANES - shift, 1), b)
        x, step = y, step // 2
    return x


def outer_kernel(tile_i, tile_j, feat_e, grad_ref, map_ref, high_ref, low_ref):
    group = LANES // feat_e
    part = tile_i // 2
    block = 2 * LANES
    rows = high_ref.shape[0] // 2
    grad = jnp.concatenate(
        [grad_ref[pl.ds(j, tile_i, stride=tile_j), :] for j in range(tile_j)], axis=0
    )
    grad_high, grad_low = split(grad)
    grad_both = jnp.concatenate([grad_high, grad_low], axis=1)
    for n in range(map_ref.shape[0] // block):
        map_high, map_low = split(map_ref[n * block : (n + 1) * block, :])
        map_both = jnp.concatenate([map_high, map_high], axis=1)
        full = product(grad_both, map_both, NT) + product(grad_high, map_low, NT)
        for m in range(block // LANES):
            for g in range(tile_j // group):
                tiles = [
                    full[(g * group + j) * tile_i :][:tile_i, m * LANES : (m + 1) * LANES]
                    for j in range(group)
                ]
                for k, tile in enumerate(swap_lane_groups(tiles, feat_e)):
                    channel = (n * (block // LANES) + m) * group + k
                    high, low = split(tile)
                    for h in range(2):
                        row = pl.ds(h * rows + channel * part, part)
                        lanes = pl.ds(g * LANES, LANES)
                        high_ref[row, lanes] = high[h * part : (h + 1) * part]
                        low_ref[row, lanes] = low[h * part : (h + 1) * part]


def load_rows(ref, first, total, pieces):
    return jnp.concatenate(
        [ref[pl.ds(first + p, total, stride=pieces), :] for p in range(pieces)], axis=1
    )


def left_kernel(total, gathered_ref, high_ref, low_ref, out_ref):
    pieces = gathered_ref.shape[0] // total
    b_high, b_low = split(load_rows(gathered_ref, 0, total, pieces))
    both = product(jnp.concatenate([b_high, b_low], axis=0), high_ref[...], NT)
    left = both[:total] + both[total:] + product(b_high, low_ref[...], NT)
    left = left * (1.0 / total)
    pieces = out_ref.shape[0] // (2 * total)
    for h in range(2):
        for p in range(pieces):
            at = (h * pieces + p) * LANES
            out_ref[pl.ds(h * total * pieces + p, total, stride=pieces), :] = left[:, at : at + LANES]


def right_kernel(total, gathered_ref, high_ref, low_ref, out_ref):
    pieces = gathered_ref.shape[0] // (2 * total)
    a_full = jnp.concatenate(
        [load_rows(gathered_ref, h * total * pieces, total, pieces) for h in range(2)], axis=1
    )
    a_high, a_low = split(a_full)
    both = product(jnp.concatenate([a_high, a_low], axis=0), high_ref[...], NN)
    right = both[:total] + both[total:] + product(a_high, low_ref[...], NN)
    right = right * (1.0 / total)
    pieces = out_ref.shape[0] // total
    for p in range(pieces):
        out_ref[pl.ds(p, total, stride=pieces), :] = right[:, p * LANES : (p + 1) * LANES]


def outer_parts(grad, mapping, feat_c, feat_e, interpret=False):
    import functools
    tile_i, tile_j, pair = grad.shape
    shape = jax.ShapeDtypeStruct((tile_i * feat_c, tile_j * feat_e), jnp.bfloat16)
    return pl.pallas_call(
        functools.partial(outer_kernel, tile_i, tile_j, feat_e),
        out_shape=(shape, shape), interpret=interpret, name="outer",
    )(grad.reshape(tile_i * tile_j, pair), mapping)


def contract(kernel, name, total, gathered, parts, rows, interpret=False):
    import functools
    return pl.pallas_call(
        functools.partial(kernel, total),
        out_shape=jax.ShapeDtypeStruct((rows, LANES), jnp.float32), interpret=interpret, name=name,
    )(gathered, *parts)


def pair_moves(rows, cols):
    half = cols // rows
    return [
        (r * cols + c, (c // half) * cols + (c % half) * rows + r)
        for r in range(rows)
        for c in range(cols)
    ]


def to_all(block, axis):
    count = lax.axis_size(axis)
    spread = jnp.broadcast_to(block[None], (count,) + block.shape)
    return lax.all_to_all(spread, axis, split_axis=0, concat_axis=0, tiled=True)


def sum_to_owner(chunks, axis):
    chunks = chunks.reshape(lax.axis_size(axis), -1, LANES)
    moved = lax.all_to_all(chunks, axis, split_axis=0, concat_axis=0, tiled=True)
    return moved.sum(axis=0)


def on_device(left, right, grad, mapping):
    rows, cols = lax.axis_size("row"), lax.axis_size("col")
    seqs, res, feat_c = left.shape
    feat_e = right.shape[2]
    total = seqs * rows
    moves = pair_moves(rows, cols)
    back = [(b, a) for a, b in moves]
    both = ("row", "col")

    left_block = left.transpose(0, 2, 1).reshape(-1, LANES)
    right_block = right.reshape(-1, LANES)
    left_all = to_all(lax.ppermute(left_block, both, moves), "col").reshape(-1, LANES)
    right_all = to_all(right_block, "row").reshape(-1, LANES)
    parts = outer_parts(grad, mapping, feat_c, feat_e)
    left_part = contract(left_kernel, "left", total, right_all, parts, left_all.shape[0])
    left_sum = lax.ppermute(sum_to_owner(left_part, "col"), both, back)
    right_part = contract(right_kernel, "right", total, left_all, parts, right_all.shape[0])
    right_sum = sum_to_owner(right_part, "row")
    grad_left = left_sum.reshape(seqs, feat_c, res).transpose(0, 2, 1)
    return (grad_left, right_sum.reshape(right.shape))


def solution(mesh):
    spec = P("row", "col", None)
    return jax.shard_map(
        on_device,
        mesh=mesh,
        in_specs=(spec, spec, spec, P()),
        out_specs=(spec, spec),
        check_vma=False,
    )
```

time: 118 us -> 92.7 us (0.79)
  the two profiles are of different devices: /device:TPU:12 before, /device:TPU:77 now
where the time goes in v2:
time: 92.7 us; the launch traced here: 92 us
  starting transfers between devices  52.3 us (56%)
  waiting for transfers between devices  24.2 us (26%)
  Pallas kernels  10.3 us (11%)
  local copies, waits for them, and re-layouts  4.57 us (5%)
    all_to_all x2, starting transfers between devices, to_all(): return lax.all_to_all(spread, axis, split_axis=0, concat_axis=0, tiled=True)  21.9 us
    all_to_all x2, starting transfers between devices, sum_to_owner(): lax.all_to_all(chunks, axis, split_axis=0, concat_axis=0, tiled=True)  16.8 us
    all_to_all x2, waiting for transfers between devices, sum_to_owner(): lax.all_to_all(chunks, axis, split_axis=0, concat_axis=0, tiled=True)  14.8 us
    ppermute x1, starting transfers between devices, on_device(): lax.ppermute(left_block, both, moves)  10.8 us
    pallas_call x2, Pallas kernels, contract(): pl.pallas_call(functools.partial(kernel, total), out_shape=jax.ShapeDtype...  5.78 us
    ppermute x1, waiting for transfers between devices, on_device(): left_sum = lax.ppermute(sum_to_owner(left_part, 'col'), both, back)  5.03 us
    pallas_call x1, Pallas kernels, outer_parts(): pl.pallas_call(functools.partial(outer_kernel, tile_i, tile_j, feat_e), o...  4.52 us
    all_to_all x2, waiting for transfers between devices, to_all(): return lax.all_to_all(spread, axis, split_axis=0, concat_axis=0, tiled=True)  3.55 us
  transfers between devices with their start and end apart: 6, of which 5 were waited for; matrix products, arithmetic and copies ran while one was open for 1% of the time, Pallas kernels for 11%

profile of v2, /device:TPU:77, one launch (start us, length us, event | category | flops | bytes accessed | tf_op | source)
XLA Modules:
  0.0 92.0 jit_solution(11129063228803961534)
XLA Ops:
  0.6 0.8 broadcast_in_dim.6
  1.5 0.7 broadcast_in_dim.14
  2.1 0.0 copy-start.2
  2.1 12.8 %all-to-all-start = ((f32[16,16,128]{2,1,0:T(8,128)}), f32[16,16,128]{2,1,0:T(8,128)S(1)}, u32[]{:S(2)}, u32[]{:S(2)}) async-start(f32[16,16,128]{2,1,0:T(8,128)} %broadcast_in_dim.14), calls=%async_computation | async-start | bytes 262144 | tf_op jit(solution)/shard_map/all_to_all | solution.py:130
  14.9 0.0 copy-done.2
  14.9 0.1 copy.6
  15.0 0.1 reshape.34
  15.1 10.8 %collective-permute-start.1 = (f32[16,128]{1,0:T(8,128)S(1)}, f32[16,128]{1,0:T(8,128)S(1)}, u32[]{:S(2)}, u32[]{:S(2)}) collective-permute-start(f32[16,128]{1,0:T(8,128)S(1)} %reshape.34), channel_id=1, source_target_pairs={{0,0},{1,16},{2,32},{3,48},{4,64},{5,80},{6,96},{7,112},{8,128},{9... | collective-permute-start | bytes 24584 | tf_op jit(solution)/shard_map/ppermute | solution.py:150
  25.9 0.8 collective-permute-done.1
  26.7 0.0 all-to-all-done
  26.7 0.0 copy-start.1
  26.7 0.7 broadcast_in_dim.15
  27.5 0.0 copy-done.1
  27.5 9.1 %all-to-all-start.2 = ((f32[32,16,128]{2,1,0:T(8,128)}), f32[32,16,128]{2,1,0:T(8,128)S(1)}, u32[]{:S(2)}, u32[]{:S(2)}) async-start(f32[32,16,128]{2,1,0:T(8,128)} %broadcast_in_dim.15), calls=%async_computation.2 | async-start | bytes 524288 | tf_op jit(solution)/shard_map/all_to_all | solution.py:130
  36.6 4.5 %outer.1 = (bf16[1024,512]{1,0:T(8,128)(2,1)}, bf16[1024,512]{1,0:T(8,128)(2,1)}) custom-call(f32[512,128]{1,0:T(8,128)} %bitcast.11, f32[1024,128]{1,0:T(8,128)} %map_ref.1), custom_call_target="tpu_custom_call" | custom-call | tf_op jit(solution)/shard_map/outer/pallas_call | solution.py:104
  41.1 3.1 %left.1 = f32[512,128]{1,0:T(8,128)} custom-call(f32[256,128]{1,0:T(8,128)} %bitcast.9, bf16[1024,512]{1,0:T(8,128)(2,1)} %get-tuple-element.4.high_ref, bf16[1024,512]{1,0:T(8,128)(2,1)} %get-tuple-element.5.low_ref), custom_call_target="tpu_custom_call" | custom-call | tf_op jit(solution)/shard_map/left/pallas_call | solution.py:112
  44.1 3.5 %all-to-all-done.2 = f32[32,16,128]{2,1,0:T(8,128)S(1)} async-done(((f32[32,16,128]{2,1,0:T(8,128)}), f32[32,16,128]{2,1,0:T(8,128)S(1)}, u32[]{:S(2)}, u32[]{:S(2)}) %all-to-all-start.2) | async-done | bytes 262176 | tf_op jit(solution)/shard_map/all_to_all | solution.py:130
  47.7 0.0 copy-start
  47.7 0.7 copy-done
  48.4 6.1 %all-to-all-start.1 = ((f32[32,16,128]{2,1,0:T(8,128)}), f32[32,16,128]{2,1,0:T(8,128)S(1)}, u32[]{:S(2)}, u32[]{:S(2)}) async-start(f32[32,16,128]{2,1,0:T(8,128)} %bitcast.8), calls=%async_computation.1 | async-start | bytes 524288 | tf_op jit(solution)/shard_map/all_to_all | solution.py:135
  54.5 2.7 %right.1 = f32[256,128]{1,0:T(8,128)} custom-call(f32[512,128]{1,0:T(8,128)} %bitcast.7, bf16[1024,512]{1,0:T(8,128)(2,1)} %get-tuple-element.4.high_ref, bf16[1024,512]{1,0:T(8,128)(2,1)} %get-tuple-element.5.low_ref), custom_call_target="tpu_custom_call" | custom-call | tf_op jit(solution)/shard_map/right/pallas_call | solution.py:112
  57.2 8.1 %all-to-all-done.1 = f32[32,16,128]{2,1,0:T(8,128)S(1)} async-done(((f32[32,16,128]{2,1,0:T(8,128)}), f32[32,16,128]{2,1,0:T(8,128)S(1)}, u32[]{:S(2)}, u32[]{:S(2)}) %all-to-all-start.1) | async-done | bytes 262176 | tf_op jit(solution)/shard_map/all_to_all | solution.py:135
  65.3 10.8 %all-to-all-start.3 = ((f32[16,16,128]{2,1,0:T(8,128)}), f32[16,16,128]{2,1,0:T(8,128)S(1)}, u32[]{:S(2)}, u32[]{:S(2)}) async-start(f32[16,16,128]{2,1,0:T(8,128)} %bitcast.10), calls=%async_computation.3 | async-start | bytes 262144 | tf_op jit(solution)/shard_map/all_to_all | solution.py:135
  76.1 2.7 %collective-permute-start = (f32[16,128]{1,0:T(8,128)S(1)}, f32[16,128]{1,0:T(8,128)S(1)}, u32[]{:S(2)}, u32[]{:S(2)}) collective-permute-start(f32[16,128]{1,0:T(8,128)S(1)} %reduce_sum.18), channel_id=1, source_target_pairs={{0,0},{16,1},{32,2},{48,3},{64,4},{80,5},{96,6},{112,7},{128,8},{1... | collective-permute-start | bytes 24584 | tf_op jit(solution)/shard_map/ppermute | solution.py:154
  78.8 6.7 %all-to-all-done.3 = f32[16,16,128]{2,1,0:T(8,128)S(1)} async-done(((f32[16,16,128]{2,1,0:T(8,128)}), f32[16,16,128]{2,1,0:T(8,128)S(1)}, u32[]{:S(2)}, u32[]{:S(2)}) %all-to-all-start.3) | async-done | bytes 131104 | tf_op jit(solution)/shard_map/all_to_all | solution.py:135
  85.5 0.7 reshape.37
  86.2 5.0 %collective-permute-done = f32[16,128]{1,0:T(8,128)S(1)} collective-permute-done((f32[16,128]{1,0:T(8,128)S(1)}, f32[16,128]{1,0:T(8,128)S(1)}, u32[]{:S(2)}, u32[]{:S(2)}) %collective-permute-start) | collective-permute-done | bytes 8224 | tf_op jit(solution)/shard_map/ppermute | solution.py:154
  91.3 0.1 reshape.33
  91.3 0.7 copy.7
  (2 shorter events, 0.1 us)
Async XLA Ops:
  2.1 12.8 %copy-start.2 = (f32[4,16,32]{2,1,0:T(8,128)S(1)}, f32[4,16,32]{2,1,0:T(8,128)}, u32[]{:S(2)}) copy-start(f32[4,16,32]{2,1,0:T(8,128)} %param.4) | copy-start | bytes 24580
  2.1 24.6 %all-to-all-start = ((f32[16,16,128]{2,1,0:T(8,128)}), f32[16,16,128]{2,1,0:T(8,128)S(1)}, u32[]{:S(2)}, u32[]{:S(2)}) async-start(f32[16,16,128]{2,1,0:T(8,128)} %broadcast_in_dim.14), calls=%async_computation | async-start | bytes 262144 | tf_op jit(solution)/shard_map/all_to_all | solution.py:130
  15.1 11.6 %collective-permute-start.1 = (f32[16,128]{1,0:T(8,128)S(1)}, f32[16,128]{1,0:T(8,128)S(1)}, u32[]{:S(2)}, u32[]{:S(2)}) collective-permute-start(f32[16,128]{1,0:T(8,128)S(1)} %reshape.34), channel_id=1, source_target_pairs={{0,0},{1,16},{2,32},{3,48},{4,64},{5,80},{6,96},{7,112},{8,128},{9... | collective-permute-start | bytes 24584 | tf_op jit(solution)/shard_map/ppermute | solution.py:150
  26.7 0.8 copy-start.1
  27.5 20.2 %all-to-all-start.2 = ((f32[32,16,128]{2,1,0:T(8,128)}), f32[32,16,128]{2,1,0:T(8,128)S(1)}, u32[]{:S(2)}, u32[]{:S(2)}) async-start(f32[32,16,128]{2,1,0:T(8,128)} %broadcast_in_dim.15), calls=%async_computation.2 | async-start | bytes 524288 | tf_op jit(solution)/shard_map/all_to_all | solution.py:130
  47.7 0.7 copy-start
  48.4 16.9 %all-to-all-start.1 = ((f32[32,16,128]{2,1,0:T(8,128)}), f32[32,16,128]{2,1,0:T(8,128)S(1)}, u32[]{:S(2)}, u32[]{:S(2)}) async-start(f32[32,16,128]{2,1,0:T(8,128)} %bitcast.8), calls=%async_computation.1 | async-start | bytes 524288 | tf_op jit(solution)/shard_map/all_to_all | solution.py:135
  65.3 20.2 %all-to-all-start.3 = ((f32[16,16,128]{2,1,0:T(8,128)}), f32[16,16,128]{2,1,0:T(8,128)S(1)}, u32[]{:S(2)}, u32[]{:S(2)}) async-start(f32[16,16,128]{2,1,0:T(8,128)} %bitcast.10), calls=%async_computation.3 | async-start | bytes 262144 | tf_op jit(solution)/shard_map/all_to_all | solution.py:135
  76.1 15.2 %collective-permute-start = (f32[16,128]{1,0:T(8,128)S(1)}, f32[16,128]{1,0:T(8,128)S(1)}, u32[]{:S(2)}, u32[]{:S(2)}) collective-permute-start(f32[16,128]{1,0:T(8,128)S(1)} %reduce_sum.18), channel_id=1, source_target_pairs={{0,0},{16,1},{32,2},{48,3},{64,4},{80,5},{96,6},{112,7},{128,8},{1... | collective-permute-start | bytes 24584 | tf_op jit(solution)/shard_map/ppermute | solution.py:154

commit v3 on v2

--- a/solution.py
+++ b/solution.py
@@ -1,3 +1,5 @@
+import functools
+
 import jax
 import jax.numpy as jnp
 from jax import lax
@@ -70,49 +72,63 @@
     )
 
 
-def left_kernel(total, gathered_ref, high_ref, low_ref, out_ref):
+def left_kernel(total, gathered_ref, block_ref, high_ref, low_ref, out_ref):
     pieces = gathered_ref.shape[0] // total
     b_high, b_low = split(load_rows(gathered_ref, 0, total, pieces))
     both = product(jnp.concatenate([b_high, b_low], axis=0), high_ref[...], NT)
     left = both[:total] + both[total:] + product(b_high, low_ref[...], NT)
     left = left * (1.0 / total)
-    pieces = out_ref.shape[0] // (2 * total)
-    for h in range(2):
-        for p in range(pieces):
-            at = (h * pieces + p) * LANES
-            out_ref[pl.ds(h * total * pieces + p, total, stride=pieces), :] = left[:, at : at + LANES]
+    turn = out_ref.shape[0] // (2 * total)
+    pieces = turn // 2
+    seqs = block_ref.shape[0] // pieces
+    for p in range(pieces):
+        mine = block_ref[pl.ds(p, seqs, stride=pieces), :]
+        mine = jnp.concatenate([mine] * (total // seqs), axis=0)
+        for h in range(2):
+            lanes = (h * pieces + p) * LANES
+            row = h * total * turn + p
+            out_ref[pl.ds(row, total, stride=turn), :] = mine
+            out_ref[pl.ds(row + pieces, total, stride=turn), :] = left[:, lanes : lanes + LANES]
 
 
-def right_kernel(total, gathered_ref, high_ref, low_ref, out_ref):
-    pieces = gathered_ref.shape[0] // (2 * total)
+def right_kernel(total, seqs, gathered_ref, high_ref, low_ref, out_ref, sum_ref):
+    turn = gathered_ref.shape[0] // (2 * total)
+    pieces = turn // 2
     a_full = jnp.concatenate(
-        [load_rows(gathered_ref, h * total * pieces, total, pieces) for h in range(2)], axis=1
+        [
+            gathered_ref[pl.ds(h * total * turn + p, total, stride=turn), :]
+            for h in range(2)
+            for p in range(pieces)
+        ],
+        axis=1,
     )
     a_high, a_low = split(a_full)
     both = product(jnp.concatenate([a_high, a_low], axis=0), high_ref[...], NN)
     right = both[:total] + both[total:] + product(a_high, low_ref[...], NN)
     right = right * (1.0 / total)
+    block = seqs * turn
+    chunks = [gathered_ref[k : k + block, :] for k in range(0, gathered_ref.shape[0], block)]
+    while len(chunks) > 1:
+        chunks = [a + b for a, b in zip(chunks[::2], chunks[1::2])]
+    for s in range(seqs):
+        sum_ref[s * pieces : (s + 1) * pieces, :] = chunks[0][s * turn + pieces : (s + 1) * turn]
     pieces = out_ref.shape[0] // total
     for p in range(pieces):
         out_ref[pl.ds(p, total, stride=pieces), :] = right[:, p * LANES : (p + 1) * LANES]
 
 
-def outer_parts(grad, mapping, feat_c, feat_e, interpret=False):
-    import functools
-    tile_i, tile_j, pair = grad.shape
-    shape = jax.ShapeDtypeStruct((tile_i * feat_c, tile_j * feat_e), jnp.bfloat16)
-    return pl.pallas_call(
-        functools.partial(outer_kernel, tile_i, tile_j, feat_e),
-        out_shape=(shape, shape), interpret=interpret, name="outer",
-    )(grad.reshape(tile_i * tile_j, pair), mapping)
+VMEM = pl.BlockSpec(memory_space=pltpu.VMEM)
 
 
-def contract(kernel, name, total, gathered, parts, rows, interpret=False):
-    import functools
+def call(kernel, name, outs, *args, interpret=False):
     return pl.pallas_call(
-        functools.partial(kernel, total),
-        out_shape=jax.ShapeDtypeStruct((rows, LANES), jnp.float32), interpret=interpret, name=name,
-    )(gathered, *parts)
+        kernel,
+        out_shape=tuple(jax.ShapeDtypeStruct(shape, dtype) for shape, dtype in outs),
+        in_specs=[VMEM] * len(args),
+        out_specs=(VMEM,) * len(outs),
+        interpret=interpret,
+        name=name,
+    )(*args)
 
 
 def pair_moves(rows, cols):
@@ -124,36 +140,43 @@
     ]
 
 
-def to_all(block, axis):
-    count = lax.axis_size(axis)
-    spread = jnp.broadcast_to(block[None], (count,) + block.shape)
-    return lax.all_to_all(spread, axis, split_axis=0, concat_axis=0, tiled=True)
+def to_each(chunks, axis):
+    chunks = chunks.reshape(lax.axis_size(axis), -1, LANES)
+    return lax.all_to_all(chunks, axis, split_axis=0, concat_axis=0, tiled=True)
 
 
-def sum_to_owner(chunks, axis):
-    chunks = chunks.reshape(lax.axis_size(axis), -1, LANES)
-    moved = lax.all_to_all(chunks, axis, split_axis=0, concat_axis=0, tiled=True)
-    return moved.sum(axis=0)
-
-
-def on_device(left, right, grad, mapping):
+def on_device(left, right, grad, mapping, interpret=False):
     rows, cols = lax.axis_size("row"), lax.axis_size("col")
     seqs, res, feat_c = left.shape
     feat_e = right.shape[2]
+    tile_i, tile_j, pair = grad.shape
     total = seqs * rows
+    f32, bf16 = jnp.float32, jnp.bfloat16
+    run = functools.partial(call, interpret=interpret)
     moves = pair_moves(rows, cols)
     back = [(b, a) for a, b in moves]
     both = ("row", "col")
 
-    left_block = left.transpose(0, 2, 1).reshape(-1, LANES)
+    left_block = lax.ppermute(left.transpose(0, 2, 1).reshape(-1, LANES), both, moves)
     right_block = right.reshape(-1, LANES)
-    left_all = to_all(lax.ppermute(left_block, both, moves), "col").reshape(-1, LANES)
-    right_all = to_all(right_block, "row").reshape(-1, LANES)
-    parts = outer_parts(grad, mapping, feat_c, feat_e)
-    left_part = contract(left_kernel, "left", total, right_all, parts, left_all.shape[0])
-    left_sum = lax.ppermute(sum_to_owner(left_part, "col"), both, back)
-    right_part = contract(right_kernel, "right", total, left_all, parts, right_all.shape[0])
-    right_sum = sum_to_owner(right_part, "row")
+    right_all = to_each(jnp.broadcast_to(right_block[None], (rows,) + right_block.shape), "row")
+    outer_shape = (tile_i * feat_c, tile_j * feat_e)
+    high, low = run(
+        functools.partial(outer_kernel, tile_i, tile_j, feat_e), "outer",
+        [(outer_shape, bf16)] * 2, grad.reshape(tile_i * tile_j, pair), mapping,
+    )
+    block_rows = left_block.shape[0]
+    (shared,) = run(
+        functools.partial(left_kernel, total), "left", [((cols * 2 * block_rows, LANES), f32)],
+        right_all.reshape(-1, LANES), left_block, high, low,
+    )
+    shared = to_each(shared, "col").reshape(-1, LANES)
+    right_part, left_sum = run(
+        functools.partial(right_kernel, total, seqs), "right",
+        [((rows * right_block.shape[0], LANES), f32), (left_block.shape, f32)], shared, high, low,
+    )
+    left_sum = lax.ppermute(left_sum, both, back)
+    right_sum = to_each(right_part, "row").sum(axis=0)
     grad_left = left_sum.reshape(seqs, feat_c, res).transpose(0, 2, 1)
     return (grad_left, right_sum.reshape(right.shape))
 

time: 92.7 us -> 85.4 us (0.921)
  the two profiles are of different devices: /device:TPU:77 before, /device:TPU:14 now
where the time goes in v3:
time: 85.4 us; the launch traced here: 84.8 us
  starting transfers between devices  34.4 us (40%)
  blocking collectives  26.6 us (31%)
  Pallas kernels  10.6 us (12%)
  waiting for transfers between devices  8.78 us (10%)
  local copies, waits for them, and re-layouts  3.78 us (4%)
    all_to_all x1, blocking collectives, to_each(): return lax.all_to_all(chunks, axis, split_axis=0, concat_axis=0, tiled=True)  26.6 us
    all_to_all x2, starting transfers between devices, to_each(): return lax.all_to_all(chunks, axis, split_axis=0, concat_axis=0, tiled=True)  20.5 us
    pallas_call x3, Pallas kernels, call(): pl.pallas_call(kernel, out_shape=tuple((jax.ShapeDtypeStruct(shape, dtype...  10.6 us
    ppermute x1, starting transfers between devices, on_device(): lax.ppermute(left.transpose(0, 2, 1).reshape(-1, LANES), both, moves)  9.29 us
    ppermute x1, waiting for transfers between devices, on_device(): left_sum = lax.ppermute(left_sum, both, back)  8.77 us
    ppermute x1, starting transfers between devices, on_device(): left_sum = lax.ppermute(left_sum, both, back)  4.58 us
  transfers between devices with their start and end apart: 4, of which 1 were waited for; matrix products, arithmetic and copies ran while one was open for 1% of the time, Pallas kernels for 5%

profile of v3, /device:TPU:14, one launch (start us, length us, event | category | flops | bytes accessed | tf_op | source)
XLA Modules:
  0.0 84.8 jit_solution(14564318984237988564)
XLA Ops:
  0.6 0.8 broadcast_in_dim.7
  1.5 0.7 broadcast_in_dim.8
  2.1 0.0 copy-start.1
  2.1 13.4 %all-to-all-start = ((f32[16,16,128]{2,1,0:T(8,128)}), f32[16,16,128]{2,1,0:T(8,128)S(1)}, u32[]{:S(2)}, u32[]{:S(2)}) async-start(f32[16,16,128]{2,1,0:T(8,128)} %broadcast_in_dim.8), calls=%async_computation | async-start | bytes 262144 | tf_op jit(solution)/shard_map/all_to_all | solution.py:145
  15.5 0.0 copy-done.1
  15.5 0.1 copy.8
  15.6 0.1 reshape.30
  15.7 9.3 %collective-permute-start = (f32[16,128]{1,0:T(8,128)S(1)}, f32[16,128]{1,0:T(8,128)S(1)}, u32[]{:S(2)}, u32[]{:S(2)}) collective-permute-start(f32[16,128]{1,0:T(8,128)S(1)} %reshape.30), channel_id=1, source_target_pairs={{0,0},{1,16},{2,32},{3,48},{4,64},{5,80},{6,96},{7,112},{8,128},{9... | collective-permute-start | bytes 24584 | tf_op jit(solution)/shard_map/ppermute | solution.py:160
  25.0 4.5 %outer.1 = (bf16[1024,512]{1,0:T(8,128)(2,1)}, bf16[1024,512]{1,0:T(8,128)(2,1)}) custom-call(f32[512,128]{1,0:T(8,128)} %bitcast.10, f32[1024,128]{1,0:T(8,128)} %map_ref.1), custom_call_target="tpu_custom_call" | custom-call | tf_op jit(solution)/shard_map/outer/pallas_call | solution.py:124
  29.5 0.0 collective-permute-done.block_ref
  29.5 0.0 copy-start.2
  29.5 0.0 all-to-all-done
  29.5 0.0 copy-start
  29.5 0.6 copy-done.2
  30.1 0.1 copy-done
  30.2 3.2 %left.1 = f32[1024,128]{1,0:T(8,128)} custom-call(f32[256,128]{1,0:T(8,128)} %bitcast.9, f32[16,128]{1,0:T(8,128)} %copy-done.2, bf16[1024,512]{1,0:T(8,128)(2,1)} %get-tuple-element.6.high_ref, bf16[1024,512]{1,0:T(8,128)(2,1)} %get-tuple-element.7.low_ref), custom_call_target="tpu_custom_call" | custom-call | tf_op jit(solution)/shard_map/left/pallas_call | solution.py:124
  33.4 26.6 %all_to_all.15 = f32[32,32,128]{2,1,0:T(8,128)} all-to-all(f32[32,32,128]{2,1,0:T(8,128)} %bitcast.8), channel_id=1, replica_groups=mesh['row'=16,'col'=32] {'col'}, dimensions={0} | all-to-all | bytes 1048576 | tf_op jit(solution)/shard_map/all_to_all | solution.py:145
  60.0 2.8 %right.1 = (f32[256,128]{1,0:T(8,128)}, f32[16,128]{1,0:T(8,128)}) custom-call(f32[1024,128]{1,0:T(8,128)} %bitcast.7, bf16[1024,512]{1,0:T(8,128)(2,1)} %get-tuple-element.6.high_ref, bf16[1024,512]{1,0:T(8,128)(2,1)} %get-tuple-element.7.low_ref), custom_call_target="tpu_custom_call" | custom-call | tf_op jit(solution)/shard_map/right/pallas_call | solution.py:124
  62.8 0.0 copy-start.3
  62.8 7.2 %all-to-all-start.2 = ((f32[16,16,128]{2,1,0:T(8,128)}), f32[16,16,128]{2,1,0:T(8,128)S(1)}, u32[]{:S(2)}, u32[]{:S(2)}) async-start(f32[16,16,128]{2,1,0:T(8,128)} %bitcast.12), calls=%async_computation.2 | async-start | bytes 262144 | tf_op jit(solution)/shard_map/all_to_all | solution.py:145
  69.9 0.0 copy-done.3
  70.0 4.6 %collective-permute-start.1 = (f32[16,128]{1,0:T(8,128)S(1)}, f32[16,128]{1,0:T(8,128)S(1)}, u32[]{:S(2)}, u32[]{:S(2)}) collective-permute-start(f32[16,128]{1,0:T(8,128)S(1)} %copy-done.3), channel_id=1, source_target_pairs={{0,0},{16,1},{32,2},{48,3},{64,4},{80,5},{96,6},{112,7},{128,8},{1... | collective-permute-start | bytes 24584 | tf_op jit(solution)/shard_map/ppermute | solution.py:178
  74.5 8.8 %collective-permute-done.1 = f32[16,128]{1,0:T(8,128)S(1)} collective-permute-done((f32[16,128]{1,0:T(8,128)S(1)}, f32[16,128]{1,0:T(8,128)S(1)}, u32[]{:S(2)}, u32[]{:S(2)}) %collective-permute-start.1) | collective-permute-done | bytes 8224 | tf_op jit(solution)/shard_map/ppermute | solution.py:178
  83.3 0.1 reshape.34
  83.4 0.7 copy.9
  84.1 0.0 all-to-all-done.2
  84.1 0.7 reshape.36
  (1 shorter events, 0.0 us)
Async XLA Ops:
  2.1 13.4 %copy-start.1 = (f32[4,16,32]{2,1,0:T(8,128)S(1)}, f32[4,16,32]{2,1,0:T(8,128)}, u32[]{:S(2)}) copy-start(f32[4,16,32]{2,1,0:T(8,128)} %param.4) | copy-start | bytes 24580
  2.1 27.4 %all-to-all-start = ((f32[16,16,128]{2,1,0:T(8,128)}), f32[16,16,128]{2,1,0:T(8,128)S(1)}, u32[]{:S(2)}, u32[]{:S(2)}) async-start(f32[16,16,128]{2,1,0:T(8,128)} %broadcast_in_dim.8), calls=%async_computation | async-start | bytes 262144 | tf_op jit(solution)/shard_map/all_to_all | solution.py:145
  15.7 13.8 %collective-permute-start = (f32[16,128]{1,0:T(8,128)S(1)}, f32[16,128]{1,0:T(8,128)S(1)}, u32[]{:S(2)}, u32[]{:S(2)}) collective-permute-start(f32[16,128]{1,0:T(8,128)S(1)} %reshape.30), channel_id=1, source_target_pairs={{0,0},{1,16},{2,32},{3,48},{4,64},{5,80},{6,96},{7,112},{8,128},{9... | collective-permute-start | bytes 24584 | tf_op jit(solution)/shard_map/ppermute | solution.py:160
  29.5 0.6 copy-start.2
  29.5 0.7 copy-start
  62.8 7.2 %copy-start.3 = (f32[16,128]{1,0:T(8,128)S(1)}, f32[16,128]{1,0:T(8,128)}, u32[]{:S(2)}) copy-start(f32[16,128]{1,0:T(8,128)} %get-tuple-element.8) | copy-start | bytes 24580
  62.8 21.3 %all-to-all-start.2 = ((f32[16,16,128]{2,1,0:T(8,128)}), f32[16,16,128]{2,1,0:T(8,128)S(1)}, u32[]{:S(2)}, u32[]{:S(2)}) async-start(f32[16,16,128]{2,1,0:T(8,128)} %bitcast.12), calls=%async_computation.2 | async-start | bytes 262144 | tf_op jit(solution)/shard_map/all_to_all | solution.py:145
  70.0 13.4 %collective-permute-start.1 = (f32[16,128]{1,0:T(8,128)S(1)}, f32[16,128]{1,0:T(8,128)S(1)}, u32[]{:S(2)}, u32[]{:S(2)}) collective-permute-start(f32[16,128]{1,0:T(8,128)S(1)} %copy-done.3), channel_id=1, source_target_pairs={{0,0},{16,1},{32,2},{48,3},{64,4},{80,5},{96,6},{112,7},{128,8},{1... | collective-permute-start | bytes 24584 | tf_op jit(solution)/shard_map/ppermute | solution.py:178

commit v4 on v3

v4 whole, which is shorter than its diff:
```python
import functools

import jax
import jax.numpy as jnp
from jax import lax
from jax.experimental import pallas as pl
from jax.experimental.pallas import tpu as pltpu
from jax.sharding import PartitionSpec as P

LANES = 128
NT = (((1,), (1,)), ((), ()))
NN = (((1,), (0,)), ((), ()))


def split(x):
    high = x.astype(jnp.bfloat16)
    return high, (x - high.astype(jnp.float32)).astype(jnp.bfloat16)


def product(a, b, dims):
    return lax.dot_general(a, b, dims, preferred_element_type=jnp.float32)


def swap_lane_groups(x):
    width = LANES // 4
    place = lax.broadcasted_iota(jnp.int32, x[0].shape, 1) // width
    front, even = place < 2, place % 2 == 0
    cross = (place == 0) | (place == 3)
    pick = jnp.where
    kept = pick(cross, x[0], x[2])
    turned = pltpu.roll(pick(cross, x[2], x[0]), 2 * width, 1)
    other = pltpu.roll(pick(front, x[3], x[1]), 2 * width, 1)
    firsts = (pick(front, kept, turned), pick(front, turned, kept))
    seconds = (pick(front, x[1], other), pick(front, other, x[3]))
    y = []
    for first, second in zip(firsts, seconds):
        turned = pltpu.roll(pick(even, second, first), width, 1)
        y += [pick(even, first, turned), pick(even, turned, second)]
    return y


def outer_kernel(
    tile_i, tile_j, feat_e, grad_hbm, map_hbm, out_ref, grad_ref, map_ref, in_sem
):
    group = LANES // feat_e
    part = tile_i // 2
    block = 2 * LANES
    steps = map_ref.shape[0] // block
    rows = out_ref.shape[0] // 4
    moved = [
        pltpu.make_async_copy(grad_hbm, grad_ref, in_sem.at[0]),
        pltpu.make_async_copy(map_hbm, map_ref, in_sem.at[1]),
    ]
    for copy in moved:
        copy.start()
    for copy in moved:
        copy.wait()
    grads = []
    for g in range(tile_j // group):
        grad = [grad_ref[pl.ds(g * group + j, tile_i, stride=tile_j), :] for j in range(group)]
        high, low = split(jnp.concatenate(grad, axis=0))
        grads.append((high, jnp.concatenate([high, low], axis=1)))
    for n in range(steps):
        map_high, map_low = split(map_ref[n * block : (n + 1) * block, :])
        map_both = jnp.concatenate([map_high, map_high], axis=1)
        for g, (grad_high, grad_both) in enumerate(grads):
            full = product(grad_both, map_both, NT) + product(grad_high, map_low, NT)
            for m in range(block // LANES):
                tiles = [
                    full[j * tile_i : (j + 1) * tile_i, m * LANES : (m + 1) * LANES]
                    for j in range(group)
                ]
                for k, tile in enumerate(swap_lane_groups(tiles)):
                    channel = (n * (block // LANES) + m) * group + k
                    for w, value in enumerate(split(tile)):
                        for h in range(2):
                            row = pl.ds((2 * w + h) * rows + channel * part, part)
                            lanes = pl.ds(g * LANES, LANES)
                            out_ref[row, lanes] = value[h * part : (h + 1) * part]


def load_rows(ref, first, total, pieces):
    return jnp.concatenate(
        [ref[pl.ds(first + p, total, stride=pieces), :] for p in range(pieces)], axis=1
    )


def left_kernel(total, gathered_ref, block_ref, outer_ref, out_ref):
    steps = 4
    pieces = gathered_ref.shape[0] // total
    b_high, b_low = split(load_rows(gathered_ref, 0, total, pieces))
    b_both = jnp.concatenate([b_high, b_low], axis=0)
    turn = out_ref.shape[0] // (2 * total)
    pieces = turn // 2
    seqs = block_ref.shape[0] // pieces
    for p in range(pieces):
        mine = block_ref[pl.ds(p, seqs, stride=pieces), :]
        mine = jnp.concatenate([mine] * (total // seqs), axis=0)
        for h in range(2):
            out_ref[pl.ds(h * total * turn + p, total, stride=turn), :] = mine
    rows = outer_ref.shape[0] // 2
    span = rows // steps
    for n in range(steps):
        both = product(b_both, outer_ref[pl.ds(n * span, span), :], NT)
        last = product(b_high, outer_ref[pl.ds(rows + n * span, span), :], NT)
        left = both[:total] + both[total:] + last
        left = left * (1.0 / total)
        for m in range(span // LANES):
            h, p = divmod(n * (span // LANES) + m, pieces)
            row = h * total * turn + pieces + p
            out_ref[pl.ds(row, total, stride=turn), :] = left[:, m * LANES : (m + 1) * LANES]


def right_kernel(total, seqs, gathered_ref, outer_ref, out_ref, sum_ref):
    turn = gathered_ref.shape[0] // (2 * total)
    pieces = turn // 2
    a_full = jnp.concatenate(
        [
            gathered_ref[pl.ds(h * total * turn + p, total, stride=turn), :]
            for h in range(2)
            for p in range(pieces)
        ],
        axis=1,
    )
    a_high, a_low = split(a_full)
    rows = outer_ref.shape[0] // 2
    both = product(jnp.concatenate([a_high, a_low], axis=0), outer_ref[:rows, :], NN)
    right = both[:total] + both[total:] + product(a_high, outer_ref[rows:, :], NN)
    right = right * (1.0 / total)
    block = seqs * turn
    chunks = [gathered_ref[k : k + block, :] for k in range(0, gathered_ref.shape[0], block)]
    while len(chunks) > 1:
        chunks = [a + b for a, b in zip(chunks[::2], chunks[1::2])]
    for s in range(seqs):
        sum_ref[s * pieces : (s + 1) * pieces, :] = chunks[0][s * turn + pieces : (s + 1) * turn]
    pieces = out_ref.shape[0] // total
    for p in range(pieces):
        out_ref[pl.ds(p, total, stride=pieces), :] = right[:, p * LANES : (p + 1) * LANES]


def pack_kernel(feat_c, feat_e, left_ref, right_ref, block_ref, spread_ref, flat_ref):
    count = block_ref.shape[0]
    group = LANES // feat_e
    pieces = [right_ref[pl.ds(g, count, stride=group), :] for g in range(group)]
    mine = jnp.concatenate(pieces, axis=1)
    for k in range(spread_ref.shape[0] // count):
        spread_ref[k * count : (k + 1) * count, :] = mine
    res = LANES * count // flat_ref.shape[0]
    for s in range(left_ref.shape[0] // res):
        flat_ref[s * feat_c : (s + 1) * feat_c, :] = left_ref[s * res : (s + 1) * res, :].T
    group = LANES // res
    pieces = [flat_ref[pl.ds(g, count, stride=group), :] for g in range(group)]
    block_ref[...] = jnp.concatenate(pieces, axis=1)


def unpack_kernel(feat_c, feat_e, sum_ref, parts_ref, left_ref, right_ref, flat_ref):
    count = sum_ref.shape[0]
    res = LANES * count // flat_ref.shape[0]
    group = LANES // res
    for g in range(group):
        flat_ref[pl.ds(g, count, stride=group), :] = sum_ref[:, g * res : (g + 1) * res]
    for s in range(left_ref.shape[0] // res):
        left_ref[s * res : (s + 1) * res, :] = flat_ref[s * feat_c : (s + 1) * feat_c, :].T
    parts = [parts_ref[k : k + count, :] for k in range(0, parts_ref.shape[0], count)]
    while len(parts) > 1:
        parts = [a + b for a, b in zip(parts[::2], parts[1::2])]
    group = LANES // feat_e
    for g in range(group):
        right_ref[pl.ds(g, count, stride=group), :] = parts[0][:, g * feat_e : (g + 1) * feat_e]


VMEM = pl.BlockSpec(memory_space=pltpu.VMEM)
ANY = pl.BlockSpec(memory_space=pl.ANY)


def call(kernel, name, outs, args, scratch=(), interpret=False):
    place = lambda x, near: pltpu.with_memory_space_constraint(x, pltpu.VMEM) if near else x
    kind = lambda near: pltpu.VMEM if near else jax.ShapeDtypeStruct
    if interpret:
        place, kind = (lambda x, near: x), (lambda near: jax.ShapeDtypeStruct)
    return pl.pallas_call(
        kernel,
        out_shape=tuple(kind(near)(shape, dtype) for (shape, dtype), near in outs),
        in_specs=[ANY if near is False else VMEM for _, near in args],
        out_specs=tuple(ANY if near is False else VMEM for _, near in outs),
        scratch_shapes=scratch,
        interpret=interpret,
        name=name,
    )(*[place(x, near) for x, near in args])


def local_outer(grad, mapping, feat_c, feat_e, **how):
    tile_i, tile_j, pair = grad.shape
    shape = (2 * tile_i * feat_c, tile_j * feat_e)
    grad = grad.reshape(tile_i * tile_j, pair)
    return call(
        functools.partial(outer_kernel, tile_i, tile_j, feat_e), "outer",
        [((shape, jnp.bfloat16), True)],
        [(grad, False), (mapping, False)],
        [
            pltpu.VMEM(grad.shape, grad.dtype), pltpu.VMEM(mapping.shape, mapping.dtype),
            pltpu.SemaphoreType.DMA((2,)),
        ],
        **how,
    )[0]


def local_left(total, gathered, block, outer, rows, **how):
    return call(
        functools.partial(left_kernel, total), "left", [(((rows, LANES), jnp.float32), True)],
        [(gathered, True), (block, True), (outer, True)], **how,
    )[0]


def local_right(total, seqs, gathered, outer, rows, block_rows, **how):
    f32 = jnp.float32
    return call(
        functools.partial(right_kernel, total, seqs), "right",
        [(((rows, LANES), f32), True), (((block_rows, LANES), f32), True)],
        [(gathered, True), (outer, True)], **how,
    )


def pack(left, right, count, **how):
    seqs, res, feat_c = left.shape
    feat_e = right.shape[2]
    rows = seqs * res * feat_c // LANES
    f32 = jnp.float32
    return call(
        functools.partial(pack_kernel, feat_c, feat_e), "pack",
        [(((rows, LANES), f32), True), (((count * rows, LANES), f32), True)],
        [(left.reshape(seqs * res, feat_c), None), (right.reshape(seqs * res, feat_e), None)],
        [pltpu.VMEM((seqs * feat_c, res), f32)], **how,
    )


def unpack(left_sum, right_parts, left, right, **how):
    seqs, res, feat_c = left.shape
    feat_e = right.shape[2]
    f32 = jnp.float32
    outs = call(
        functools.partial(unpack_kernel, feat_c, feat_e), "unpack",
        [(((seqs * res, feat_c), f32), None), (((seqs * res, feat_e), f32), None)],
        [(left_sum, True), (right_parts, True)],
        [pltpu.VMEM((seqs * feat_c, res), f32)], **how,
    )
    return outs[0].reshape(left.shape), outs[1].reshape(right.shape)


def pair_moves(rows, cols):
    half = cols // rows
    return [
        (r * cols + c, (c // half) * cols + (c % half) * rows + r)
        for r in range(rows)
        for c in range(cols)
    ]


def to_each(chunks, axis):
    chunks = chunks.reshape(lax.axis_size(axis), -1, LANES)
    return lax.all_to_all(chunks, axis, split_axis=0, concat_axis=0, tiled=True)


def on_device(left, right, grad, mapping):
    rows, cols = lax.axis_size("row"), lax.axis_size("col")
    seqs, res, feat_c = left.shape
    feat_e = right.shape[2]
    total = seqs * rows
    moves = pair_moves(rows, cols)
    back = [(b, a) for a, b in moves]
    both = ("row", "col")

    left_block, right_spread = pack(left, right, rows)
    block_rows = left_block.shape[0]
    left_block = lax.ppermute(left_block, both, moves)
    right_all = to_each(right_spread, "row").reshape(-1, LANES)
    outer = local_outer(grad, mapping, feat_c, feat_e)
    shared = local_left(total, right_all, left_block, outer, cols * 2 * block_rows)
    shared = to_each(shared, "col").reshape(-1, LANES)
    right_part, left_sum = local_right(
        total, seqs, shared, outer, right_spread.shape[0], block_rows
    )
    left_sum = lax.ppermute(left_sum, both, back)
    right_parts = to_each(right_part, "row").reshape(-1, LANES)
    return unpack(left_sum, right_parts, left, right)


def solution(mesh):
    spec = P("row", "col", None)
    return jax.shard_map(
        on_device,
        mesh=mesh,
        in_specs=(spec, spec, spec, P()),
        out_specs=(spec, spec),
        check_vma=False,
    )
```

time: 85.4 us -> 79 us (0.925)
  local copies, waits for them, and re-layouts: 3.78 us -> 0 us
  Pallas kernels: 10.6 us -> 6.92 us
  blocking collectives: 26.6 us -> 28.1 us
    pallas_call x3 -> x5, Pallas kernels: 10.6 us -> 6.92 us  [call(): pl.pallas_call(kernel, out_shape=tuple((kind(near)(shape, dtype) for (sha...]
    all_to_all x1, blocking collectives: 26.6 us -> 28.1 us  [to_each(): return lax.all_to_all(chunks, axis, split_axis=0, concat_axis=0, tiled=True)]
    broadcast_in_dim x2 -> x0, local copies, waits for them, and re-layouts: 1.5 us -> none  [on_device(): jnp.broadcast_to(right_block[None], (rows,) + right_block.shape)]
    unnamed x9 -> x0, local copies, waits for them, and re-layouts: 1.35 us -> none
  transfers between devices with their start and end apart: 4 -> 4, of which waited for: 1 -> 1; matrix products, arithmetic and copies ran while one was open for 1% -> 0% of each run, Pallas kernels for 5% -> 3%
where the time goes in v4:
time: 79 us; the launch traced here: 78.6 us
  starting transfers between devices  34.1 us (43%)
  blocking collectives  28.1 us (36%)
  waiting for transfers between devices  8.78 us (11%)
  Pallas kernels  6.92 us (9%)
    all_to_all x1, blocking collectives, to_each(): return lax.all_to_all(chunks, axis, split_axis=0, concat_axis=0, tiled=True)  28.1 us
    all_to_all x2, starting transfers between devices, to_each(): return lax.all_to_all(chunks, axis, split_axis=0, concat_axis=0, tiled=True)  20.3 us
    ppermute x1, starting transfers between devices, on_device(): left_block = lax.ppermute(left_block, both, moves)  9.29 us
    ppermute x1, waiting for transfers between devices, on_device(): left_sum = lax.ppermute(left_sum, both, back)  8.77 us
    pallas_call x5, Pallas kernels, call(): pl.pallas_call(kernel, out_shape=tuple((kind(near)(shape, dtype) for (sha...  6.92 us
    ppermute x1, starting transfers between devices, on_device(): left_sum = lax.ppermute(left_sum, both, back)  4.57 us
  transfers between devices with their start and end apart: 4, of which 1 were waited for; matrix products, arithmetic and copies ran while one was open for 0% of the time, Pallas kernels for 3%

profile of v4, /device:TPU:14, one launch (start us, length us, event | category | flops | bytes accessed | tf_op | source)
XLA Modules:
  0.0 78.6 jit_solution(10492225416242871440)
XLA Ops:
  0.6 1.5 %pack.1 = (f32[16,128]{1,0:T(8,128)S(1)}, f32[256,128]{1,0:T(8,128)}) custom-call(f32[64,32]{1,0:T(8,128)} %bitcast.16, f32[64,32]{1,0:T(8,128)} %bitcast.17), custom_call_target="tpu_custom_call" | custom-call | tf_op jit(solution)/shard_map/pack/pallas_call | solution.py:181
  2.2 13.2 %all-to-all-start = ((f32[16,16,128]{2,1,0:T(8,128)}), f32[16,16,128]{2,1,0:T(8,128)S(1)}, u32[]{:S(2)}, u32[]{:S(2)}) async-start(f32[16,16,128]{2,1,0:T(8,128)} %bitcast.2), calls=%async_computation | async-start | bytes 262144 | tf_op jit(solution)/shard_map/all_to_all | solution.py:261
  15.4 9.3 %collective-permute-start = (f32[16,128]{1,0:T(8,128)S(1)}, f32[16,128]{1,0:T(8,128)S(1)}, u32[]{:S(2)}, u32[]{:S(2)}) collective-permute-start(f32[16,128]{1,0:T(8,128)S(1)} %get-tuple-element.9), channel_id=1, source_target_pairs={{0,0},{1,16},{2,32},{3,48},{4,64},{5,80},{6,96},{7,112},{8,128},{9... | collective-permute-start | bytes 24584 | tf_op jit(solution)/shard_map/ppermute | solution.py:275
  24.7 2.7 %outer.1.outer_ref = bf16[2048,512]{1,0:T(8,128)(2,1)S(1)} custom-call(f32[512,128]{1,0:T(8,128)} %bitcast.15, f32[1024,128]{1,0:T(8,128)} %map_hbm.1), custom_call_target="tpu_custom_call" | custom-call | tf_op jit(solution)/shard_map/outer/pallas_call | solution.py:181
  27.4 0.0 collective-permute-done.block_ref
  27.4 0.0 all-to-all-done
  27.4 0.8 %left.1 = f32[1024,128]{1,0:T(8,128)S(1)} custom-call(f32[256,128]{1,0:T(8,128)S(1)} %bitcast.14, f32[16,128]{1,0:T(8,128)S(1)} %collective-permute-done.block_ref, bf16[2048,512]{1,0:T(8,128)(2,1)S(1)} %outer.1.outer_ref), custom_call_target="tpu_custom_call" | custom-call | tf_op jit(solution)/shard_map/left/pallas_call | solution.py:181
  28.2 28.1 %all_to_all.15 = f32[32,32,128]{2,1,0:T(8,128)S(1)} all-to-all(f32[32,32,128]{2,1,0:T(8,128)S(1)} %bitcast.12), channel_id=1, replica_groups=mesh['row'=16,'col'=32] {'col'}, dimensions={0} | all-to-all | bytes 1048576 | tf_op jit(solution)/shard_map/all_to_all | solution.py:261
  56.3 1.1 %right.1 = (f32[256,128]{1,0:T(8,128)}, f32[16,128]{1,0:T(8,128)S(1)}) custom-call(f32[1024,128]{1,0:T(8,128)S(1)} %bitcast.11, bf16[2048,512]{1,0:T(8,128)(2,1)S(1)} %outer.1.outer_ref), custom_call_target="tpu_custom_call" | custom-call | tf_op jit(solution)/shard_map/right/pallas_call | solution.py:181
  57.4 7.0 %all-to-all-start.2 = ((f32[16,16,128]{2,1,0:T(8,128)}), f32[16,16,128]{2,1,0:T(8,128)S(1)}, u32[]{:S(2)}, u32[]{:S(2)}) async-start(f32[16,16,128]{2,1,0:T(8,128)} %bitcast.7), calls=%async_computation.2 | async-start | bytes 262144 | tf_op jit(solution)/shard_map/all_to_all | solution.py:261
  64.5 4.6 %collective-permute-start.1 = (f32[16,128]{1,0:T(8,128)S(1)}, f32[16,128]{1,0:T(8,128)S(1)}, u32[]{:S(2)}, u32[]{:S(2)}) collective-permute-start(f32[16,128]{1,0:T(8,128)S(1)} %get-tuple-element.10), channel_id=1, source_target_pairs={{0,0},{16,1},{32,2},{48,3},{64,4},{80,5},{96,6},{112,7},{128,8},{1... | collective-permute-start | bytes 24584 | tf_op jit(solution)/shard_map/ppermute | solution.py:283
  69.1 8.8 %collective-permute-done.1.sum_ref = f32[16,128]{1,0:T(8,128)S(1)} collective-permute-done((f32[16,128]{1,0:T(8,128)S(1)}, f32[16,128]{1,0:T(8,128)S(1)}, u32[]{:S(2)}, u32[]{:S(2)}) %collective-permute-start.1) | collective-permute-done | bytes 8224 | tf_op jit(solution)/shard_map/ppermute | solution.py:283
  77.8 0.0 all-to-all-done.2
  77.8 0.8 %unpack.1 = (f32[64,32]{1,0:T(8,128)}, f32[64,32]{1,0:T(8,128)}) custom-call(f32[16,128]{1,0:T(8,128)S(1)} %collective-permute-done.1.sum_ref, f32[256,128]{1,0:T(8,128)S(1)} %bitcast.13), custom_call_target="tpu_custom_call" | custom-call | tf_op jit(solution)/shard_map/unpack/pallas_call | solution.py:181
Async XLA Ops:
  2.2 25.2 %all-to-all-start = ((f32[16,16,128]{2,1,0:T(8,128)}), f32[16,16,128]{2,1,0:T(8,128)S(1)}, u32[]{:S(2)}, u32[]{:S(2)}) async-start(f32[16,16,128]{2,1,0:T(8,128)} %bitcast.2), calls=%async_computation | async-start | bytes 262144 | tf_op jit(solution)/shard_map/all_to_all | solution.py:261
  15.4 12.0 %collective-permute-start = (f32[16,128]{1,0:T(8,128)S(1)}, f32[16,128]{1,0:T(8,128)S(1)}, u32[]{:S(2)}, u32[]{:S(2)}) collective-permute-start(f32[16,128]{1,0:T(8,128)S(1)} %get-tuple-element.9), channel_id=1, source_target_pairs={{0,0},{1,16},{2,32},{3,48},{4,64},{5,80},{6,96},{7,112},{8,128},{9... | collective-permute-start | bytes 24584 | tf_op jit(solution)/shard_map/ppermute | solution.py:275
  57.4 20.4 %all-to-all-start.2 = ((f32[16,16,128]{2,1,0:T(8,128)}), f32[16,16,128]{2,1,0:T(8,128)S(1)}, u32[]{:S(2)}, u32[]{:S(2)}) async-start(f32[16,16,128]{2,1,0:T(8,128)} %bitcast.7), calls=%async_computation.2 | async-start | bytes 262144 | tf_op jit(solution)/shard_map/all_to_all | solution.py:261
  64.5 13.3 %collective-permute-start.1 = (f32[16,128]{1,0:T(8,128)S(1)}, f32[16,128]{1,0:T(8,128)S(1)}, u32[]{:S(2)}, u32[]{:S(2)}) collective-permute-start(f32[16,128]{1,0:T(8,128)S(1)} %get-tuple-element.10), channel_id=1, source_target_pairs={{0,0},{16,1},{32,2},{48,3},{64,4},{80,5},{96,6},{112,7},{128,8},{1... | collective-permute-start | bytes 24584 | tf_op jit(solution)/shard_map/ppermute | solution.py:283

commit v5 on v4

--- a/solution.py
+++ b/solution.py
@@ -1,15 +1,49 @@
 import functools
+import itertools
 
 import jax
 import jax.numpy as jnp
+import numpy as np
 from jax import lax
 from jax.experimental import pallas as pl
 from jax.experimental.pallas import tpu as pltpu
 from jax.sharding import PartitionSpec as P
 
+
 LANES = 128
 NT = (((1,), (1,)), ((), ()))
 NN = (((1,), (0,)), ((), ()))
+
+
+SIDES = (4, 2, 2, 8, 4)
+
+
+def steps_along_y(far_z, turns_x):
+    pick = jnp.where if isinstance(far_z, jax.Array) else lambda c, a, b: a if c else b
+    near = pick(turns_x == 0, 4, pick(turns_x == 1, 3, pick(turns_x == 2, 6, 5)))
+    far = pick(turns_x == 0, 2, pick(turns_x == 1, 1, pick(turns_x == 2, 0, 7)))
+    return pick(far_z == 1, far, near)
+
+
+def place_along_y(x, high, from_x, from_high):
+    return (2 * x + high + steps_along_y(from_high ^ high, (from_x - x) % 4)) % 8
+
+
+def pair_moves():
+    pairs = []
+    for from_x, from_high, from_core, y, z in itertools.product(*map(range, SIDES)):
+        x, high, core, half = y // 2, y % 2, z // 2, z % 2
+        to_y = place_along_y(x, high, from_x, from_high)
+        source = np.ravel_multi_index((from_x, from_high, from_core, y, z), SIDES)
+        target = np.ravel_multi_index((x, high, core, to_y, 2 * half + from_core), SIDES)
+        pairs.append((int(source), int(target)))
+    return pairs
+
+
+def groups_along_y():
+    row = lax.axis_index("row")
+    x, high = row // 4, (row // 2) % 2
+    return [place_along_y(x, high, from_x, from_high) for from_x in range(4) for from_high in range(2)]
 
 
 def split(x):
@@ -85,7 +119,7 @@
     )
 
 
-def left_kernel(total, gathered_ref, block_ref, outer_ref, out_ref):
+def left_kernel(total, groups, gathered_ref, block_ref, outer_ref, out_ref):
     steps = 4
     pieces = gathered_ref.shape[0] // total
     b_high, b_low = split(load_rows(gathered_ref, 0, total, pieces))
@@ -98,6 +132,8 @@
         mine = jnp.concatenate([mine] * (total // seqs), axis=0)
         for h in range(2):
             out_ref[pl.ds(h * total * turn + p, total, stride=turn), :] = mine
+    places = groups()
+    tall = total // len(places)
     rows = outer_ref.shape[0] // 2
     span = rows // steps
     for n in range(steps):
@@ -107,21 +143,27 @@
         left = left * (1.0 / total)
         for m in range(span // LANES):
             h, p = divmod(n * (span // LANES) + m, pieces)
-            row = h * total * turn + pieces + p
-            out_ref[pl.ds(row, total, stride=turn), :] = left[:, m * LANES : (m + 1) * LANES]
-
-
-def right_kernel(total, seqs, gathered_ref, outer_ref, out_ref, sum_ref):
+            for g, place in enumerate(places):
+                row = pl.multiple_of(place * (2 * tall * turn), 2 * tall * turn) + h * tall * turn + pieces + p
+                out_ref[pl.ds(row, tall, stride=turn), :] = left[
+                    g * tall : (g + 1) * tall, m * LANES : (m + 1) * LANES
+                ]
+
+
+def right_kernel(total, seqs, groups, gathered_ref, outer_ref, out_ref, sum_ref):
     turn = gathered_ref.shape[0] // (2 * total)
     pieces = turn // 2
-    a_full = jnp.concatenate(
-        [
-            gathered_ref[pl.ds(h * total * turn + p, total, stride=turn), :]
-            for h in range(2)
-            for p in range(pieces)
-        ],
-        axis=1,
-    )
+    places = groups()
+    tall = total // len(places)
+
+    def load(h, p):
+        rows = [
+            pl.multiple_of(place * (2 * tall * turn), 2 * tall * turn) + h * tall * turn + p
+            for place in places
+        ]
+        return jnp.concatenate([gathered_ref[pl.ds(r, tall, stride=turn), :] for r in rows], axis=0)
+
+    a_full = jnp.concatenate([load(h, p) for h in range(2) for p in range(pieces)], axis=1)
     a_high, a_low = split(a_full)
     rows = outer_ref.shape[0] // 2
     both = product(jnp.concatenate([a_high, a_low], axis=0), outer_ref[:rows, :], NN)
@@ -173,7 +215,7 @@
 ANY = pl.BlockSpec(memory_space=pl.ANY)
 
 
-def call(kernel, name, outs, args, scratch=(), interpret=False):
+def call(kernel, outs, args, scratch=(), interpret=False):
     place = lambda x, near: pltpu.with_memory_space_constraint(x, pltpu.VMEM) if near else x
     kind = lambda near: pltpu.VMEM if near else jax.ShapeDtypeStruct
     if interpret:
@@ -185,7 +227,6 @@
         out_specs=tuple(ANY if near is False else VMEM for _, near in outs),
         scratch_shapes=scratch,
         interpret=interpret,
-        name=name,
     )(*[place(x, near) for x, near in args])
 
 
@@ -194,7 +235,7 @@
     shape = (2 * tile_i * feat_c, tile_j * feat_e)
     grad = grad.reshape(tile_i * tile_j, pair)
     return call(
-        functools.partial(outer_kernel, tile_i, tile_j, feat_e), "outer",
+        functools.partial(outer_kernel, tile_i, tile_j, feat_e),
         [((shape, jnp.bfloat16), True)],
         [(grad, False), (mapping, False)],
         [
@@ -205,17 +246,17 @@
     )[0]
 
 
-def local_left(total, gathered, block, outer, rows, **how):
+def local_left(total, gathered, block, outer, rows, groups=groups_along_y, **how):
     return call(
-        functools.partial(left_kernel, total), "left", [(((rows, LANES), jnp.float32), True)],
+        functools.partial(left_kernel, total, groups), [(((rows, LANES), jnp.float32), True)],
         [(gathered, True), (block, True), (outer, True)], **how,
     )[0]
 
 
-def local_right(total, seqs, gathered, outer, rows, block_rows, **how):
+def local_right(total, seqs, gathered, outer, rows, block_rows, groups=groups_along_y, **how):
     f32 = jnp.float32
     return call(
-        functools.partial(right_kernel, total, seqs), "right",
+        functools.partial(right_kernel, total, seqs, groups),
         [(((rows, LANES), f32), True), (((block_rows, LANES), f32), True)],
         [(gathered, True), (outer, True)], **how,
     )
@@ -227,7 +268,7 @@
     rows = seqs * res * feat_c // LANES
     f32 = jnp.float32
     return call(
-        functools.partial(pack_kernel, feat_c, feat_e), "pack",
+        functools.partial(pack_kernel, feat_c, feat_e),
         [(((rows, LANES), f32), True), (((count * rows, LANES), f32), True)],
         [(left.reshape(seqs * res, feat_c), None), (right.reshape(seqs * res, feat_e), None)],
         [pltpu.VMEM((seqs * feat_c, res), f32)], **how,
@@ -239,7 +280,7 @@
     feat_e = right.shape[2]
     f32 = jnp.float32
     outs = call(
-        functools.partial(unpack_kernel, feat_c, feat_e), "unpack",
+        functools.partial(unpack_kernel, feat_c, feat_e),
         [(((seqs * res, feat_c), f32), None), (((seqs * res, feat_e), f32), None)],
         [(left_sum, True), (right_parts, True)],
         [pltpu.VMEM((seqs * feat_c, res), f32)], **how,
@@ -247,26 +288,17 @@
     return outs[0].reshape(left.shape), outs[1].reshape(right.shape)
 
 
-def pair_moves(rows, cols):
-    half = cols // rows
-    return [
-        (r * cols + c, (c // half) * cols + (c % half) * rows + r)
-        for r in range(rows)
-        for c in range(cols)
-    ]
-
-
 def to_each(chunks, axis):
     chunks = chunks.reshape(lax.axis_size(axis), -1, LANES)
     return lax.all_to_all(chunks, axis, split_axis=0, concat_axis=0, tiled=True)
 
 
-def on_device(left, right, grad, mapping):
+def compute(left, right, grad, mapping):
     rows, cols = lax.axis_size("row"), lax.axis_size("col")
-    seqs, res, feat_c = left.shape
+    seqs, _, feat_c = left.shape
     feat_e = right.shape[2]
     total = seqs * rows
-    moves = pair_moves(rows, cols)
+    moves = pair_moves()
     back = [(b, a) for a, b in moves]
     both = ("row", "col")
 
@@ -288,7 +320,7 @@
 def solution(mesh):
     spec = P("row", "col", None)
     return jax.shard_map(
-        on_device,
+        compute,
         mesh=mesh,
         in_specs=(spec, spec, spec, P()),
         out_specs=(spec, spec),

time: 79 us -> 78.6 us (level)
  waiting for transfers between devices: 8.78 us -> 9.92 us
  blocking collectives: 28.1 us -> 27 us
    ppermute x2, starting transfers between devices: 13.9 us -> 10.5 us  [the longest x1 7.15 us: compute(): left_block = lax.ppermute(left_block, both, moves)]
    all_to_all x2, starting transfers between devices: 20.3 us -> 23.2 us  [to_each(): return lax.all_to_all(chunks, axis, split_axis=0, concat_axis=0, tiled=True)]
    all_to_all x1, blocking collectives: 28.1 us -> 27 us  [to_each(): return lax.all_to_all(chunks, axis, split_axis=0, concat_axis=0, tiled=True)]
    ppermute x2, waiting for transfers between devices: 8.78 us -> 9.92 us  [the longest x1 9.1 us: compute(): left_sum = lax.ppermute(left_sum, both, back)]
  transfers between devices with their start and end apart: 4 -> 4, of which waited for: 1 -> 2; matrix products, arithmetic and copies ran while one was open for 0% -> 0% of each run, Pallas kernels for 3% -> 3%
where the time goes in v5:
time: 78.6 us; the launch traced here: 78.1 us
  starting transfers between devices  33.7 us (43%)
  blocking collectives  27 us (34%)
  waiting for transfers between devices  9.92 us (13%)
  Pallas kernels  6.94 us (9%)
    all_to_all x1, blocking collectives, to_each(): return lax.all_to_all(chunks, axis, split_axis=0, concat_axis=0, tiled=True)  27 us
    all_to_all x2, starting transfers between devices, to_each(): return lax.all_to_all(chunks, axis, split_axis=0, concat_axis=0, tiled=True)  23.2 us
    ppermute x1, waiting for transfers between devices, compute(): left_sum = lax.ppermute(left_sum, both, back)  9.1 us
    ppermute x1, starting transfers between devices, compute(): left_block = lax.ppermute(left_block, both, moves)  7.15 us
    pallas_call x5, Pallas kernels, call(): pl.pallas_call(kernel, out_shape=tuple((kind(near)(shape, dtype) for (sha...  6.94 us
    ppermute x1, starting transfers between devices, compute(): left_sum = lax.ppermute(left_sum, both, back)  3.34 us
  transfers between devices with their start and end apart: 4, of which 2 were waited for; matrix products, arithmetic and copies ran while one was open for 0% of the time, Pallas kernels for 3%

profile of v5, /device:TPU:14, one launch (start us, length us, event | category | flops | bytes accessed | tf_op | source)
XLA Modules:
  0.0 78.1 jit_solution(3167833042989154689)
XLA Ops:
  0.6 1.5 %shard_map.59 = (f32[16,128]{1,0:T(8,128)S(1)}, f32[256,128]{1,0:T(8,128)}) custom-call(f32[64,32]{1,0:T(8,128)} %bitcast.16, f32[64,32]{1,0:T(8,128)} %bitcast.17), custom_call_target="tpu_custom_call" | custom-call | tf_op jit(solution)/shard_map/pallas_call | solution.py:223
  2.2 13.2 %all-to-all-start = ((f32[16,16,128]{2,1,0:T(8,128)}), f32[16,16,128]{2,1,0:T(8,128)S(1)}, u32[]{:S(2)}, u32[]{:S(2)}) async-start(f32[16,16,128]{2,1,0:T(8,128)} %bitcast.2), calls=%async_computation | async-start | bytes 262144 | tf_op jit(solution)/shard_map/all_to_all | solution.py:293
  15.4 7.1 %collective-permute-start = (f32[16,128]{1,0:T(8,128)S(1)}, f32[16,128]{1,0:T(8,128)S(1)}, u32[]{:S(2)}, u32[]{:S(2)}) collective-permute-start(f32[16,128]{1,0:T(8,128)S(1)} %get-tuple-element.9), channel_id=1, source_target_pairs={{0,16},{1,18},{2,48},{3,50},{4,76},{5,78},{6,108},{7,110},{8,156},... | collective-permute-start | bytes 24584 | tf_op jit(solution)/shard_map/ppermute | solution.py:307
  22.6 2.7 %shard_map.60.outer_ref = bf16[2048,512]{1,0:T(8,128)(2,1)S(1)} custom-call(f32[512,128]{1,0:T(8,128)} %bitcast.15, f32[1024,128]{1,0:T(8,128)} %map_hbm.1), custom_call_target="tpu_custom_call" | custom-call | tf_op jit(solution)/shard_map/pallas_call | solution.py:223
  25.2 0.8 %collective-permute-done.block_ref = f32[16,128]{1,0:T(8,128)S(1)} collective-permute-done((f32[16,128]{1,0:T(8,128)S(1)}, f32[16,128]{1,0:T(8,128)S(1)}, u32[]{:S(2)}, u32[]{:S(2)}) %collective-permute-start) | collective-permute-done | bytes 8224 | tf_op jit(solution)/shard_map/ppermute | solution.py:307
  26.1 0.0 all-to-all-done
  26.1 0.8 %shard_map.61 = f32[1024,128]{1,0:T(8,128)S(1)} custom-call(f32[256,128]{1,0:T(8,128)S(1)} %bitcast.14, f32[16,128]{1,0:T(8,128)S(1)} %collective-permute-done.block_ref, bf16[2048,512]{1,0:T(8,128)(2,1)S(1)} %shard_map.60.outer_ref), custom_call_target="tpu_custom_call" | custom-call | tf_op jit(solution)/shard_map/pallas_call | solution.py:223
  26.9 27.0 %all_to_all.15 = f32[32,32,128]{2,1,0:T(8,128)S(1)} all-to-all(f32[32,32,128]{2,1,0:T(8,128)S(1)} %bitcast.12), channel_id=1, replica_groups=mesh['row'=16,'col'=32] {'col'}, dimensions={0} | all-to-all | bytes 1048576 | tf_op jit(solution)/shard_map/all_to_all | solution.py:293
  53.9 1.1 %shard_map.62 = (f32[256,128]{1,0:T(8,128)}, f32[16,128]{1,0:T(8,128)S(1)}) custom-call(f32[1024,128]{1,0:T(8,128)S(1)} %bitcast.11, bf16[2048,512]{1,0:T(8,128)(2,1)S(1)} %shard_map.60.outer_ref), custom_call_target="tpu_custom_call" | custom-call | tf_op jit(solution)/shard_map/pallas_call | solution.py:223
  55.0 9.9 %all-to-all-start.2 = ((f32[16,16,128]{2,1,0:T(8,128)}), f32[16,16,128]{2,1,0:T(8,128)S(1)}, u32[]{:S(2)}, u32[]{:S(2)}) async-start(f32[16,16,128]{2,1,0:T(8,128)} %bitcast.7), calls=%async_computation.2 | async-start | bytes 262144 | tf_op jit(solution)/shard_map/all_to_all | solution.py:293
  64.9 3.3 %collective-permute-start.1 = (f32[16,128]{1,0:T(8,128)S(1)}, f32[16,128]{1,0:T(8,128)S(1)}, u32[]{:S(2)}, u32[]{:S(2)}) collective-permute-start(f32[16,128]{1,0:T(8,128)S(1)} %get-tuple-element.10), channel_id=1, source_target_pairs={{16,0},{18,1},{48,2},{50,3},{76,4},{78,5},{108,6},{110,7},{156,8},... | collective-permute-start | bytes 24584 | tf_op jit(solution)/shard_map/ppermute | solution.py:315
  68.2 9.1 %collective-permute-done.1.sum_ref = f32[16,128]{1,0:T(8,128)S(1)} collective-permute-done((f32[16,128]{1,0:T(8,128)S(1)}, f32[16,128]{1,0:T(8,128)S(1)}, u32[]{:S(2)}, u32[]{:S(2)}) %collective-permute-start.1) | collective-permute-done | bytes 8224 | tf_op jit(solution)/shard_map/ppermute | solution.py:315
  77.3 0.0 all-to-all-done.2
  77.3 0.8 %shard_map.63 = (f32[64,32]{1,0:T(8,128)}, f32[64,32]{1,0:T(8,128)}) custom-call(f32[16,128]{1,0:T(8,128)S(1)} %collective-permute-done.1.sum_ref, f32[256,128]{1,0:T(8,128)S(1)} %bitcast.13), custom_call_target="tpu_custom_call" | custom-call | tf_op jit(solution)/shard_map/pallas_call | solution.py:223
Async XLA Ops:
  2.2 23.9 %all-to-all-start = ((f32[16,16,128]{2,1,0:T(8,128)}), f32[16,16,128]{2,1,0:T(8,128)S(1)}, u32[]{:S(2)}, u32[]{:S(2)}) async-start(f32[16,16,128]{2,1,0:T(8,128)} %bitcast.2), calls=%async_computation | async-start | bytes 262144 | tf_op jit(solution)/shard_map/all_to_all | solution.py:293
  15.4 10.7 %collective-permute-start = (f32[16,128]{1,0:T(8,128)S(1)}, f32[16,128]{1,0:T(8,128)S(1)}, u32[]{:S(2)}, u32[]{:S(2)}) collective-permute-start(f32[16,128]{1,0:T(8,128)S(1)} %get-tuple-element.9), channel_id=1, source_target_pairs={{0,16},{1,18},{2,48},{3,50},{4,76},{5,78},{6,108},{7,110},{8,156},... | collective-permute-start | bytes 24584 | tf_op jit(solution)/shard_map/ppermute | solution.py:307
  55.0 22.4 %all-to-all-start.2 = ((f32[16,16,128]{2,1,0:T(8,128)}), f32[16,16,128]{2,1,0:T(8,128)S(1)}, u32[]{:S(2)}, u32[]{:S(2)}) async-start(f32[16,16,128]{2,1,0:T(8,128)} %bitcast.7), calls=%async_computation.2 | async-start | bytes 262144 | tf_op jit(solution)/shard_map/all_to_all | solution.py:293
  64.9 12.4 %collective-permute-start.1 = (f32[16,128]{1,0:T(8,128)S(1)}, f32[16,128]{1,0:T(8,128)S(1)}, u32[]{:S(2)}, u32[]{:S(2)}) collective-permute-start(f32[16,128]{1,0:T(8,128)S(1)} %get-tuple-element.10), channel_id=1, source_target_pairs={{16,0},{18,1},{48,2},{50,3},{76,4},{78,5},{108,6},{110,7},{156,8},... | collective-permute-start | bytes 24584 | tf_op jit(solution)/shard_map/ppermute | solution.py:315

commit v6 on v5

--- a/solution.py
+++ b/solution.py
@@ -7,6 +7,7 @@
 from jax import lax
 from jax.experimental import pallas as pl
 from jax.experimental.pallas import tpu as pltpu
+from jax.sharding import Mesh
 from jax.sharding import PartitionSpec as P
 
 
@@ -15,35 +16,56 @@
 NN = (((1,), (0,)), ((), ()))
 
 
-SIDES = (4, 2, 2, 8, 4)
+SIDES = {"x": 4, "high": 2, "core": 2, "y": 8, "low": 4}
+ALL = tuple(SIDES)
+ROW = ("core", "x", "high")
+NEAR = ("core", "x")
+COL = ("low", "y")
 
 
 def steps_along_y(far_z, turns_x):
-    pick = jnp.where if isinstance(far_z, jax.Array) else lambda c, a, b: a if c else b
+    pick = jnp.where if isinstance(turns_x, jax.Array) else lambda c, a, b: a if c else b
     near = pick(turns_x == 0, 4, pick(turns_x == 1, 3, pick(turns_x == 2, 6, 5)))
     far = pick(turns_x == 0, 2, pick(turns_x == 1, 1, pick(turns_x == 2, 0, 7)))
     return pick(far_z == 1, far, near)
 
 
-def place_along_y(x, high, from_x, from_high):
-    return (2 * x + high + steps_along_y(from_high ^ high, (from_x - x) % 4)) % 8
+def place_along_y(x, high, from_x, other):
+    return (2 * x + high + steps_along_y(other, (from_x - x) % 4)) % 8
 
 
 def pair_moves():
     pairs = []
-    for from_x, from_high, from_core, y, z in itertools.product(*map(range, SIDES)):
+    for from_x, from_high, from_core, y, z in itertools.product(*map(range, SIDES.values())):
         x, high, core, half = y // 2, y % 2, z // 2, z % 2
-        to_y = place_along_y(x, high, from_x, from_high)
-        source = np.ravel_multi_index((from_x, from_high, from_core, y, z), SIDES)
-        target = np.ravel_multi_index((x, high, core, to_y, 2 * half + from_core), SIDES)
+        to_y = place_along_y(x, high, from_x, from_high ^ high)
+        source = np.ravel_multi_index((from_x, from_high, from_core, y, z), tuple(SIDES.values()))
+        target = np.ravel_multi_index((x, high, core, to_y, 2 * half + from_core), tuple(SIDES.values()))
         pairs.append((int(source), int(target)))
     return pairs
 
 
-def groups_along_y():
-    row = lax.axis_index("row")
-    x, high = row // 4, (row // 2) % 2
-    return [place_along_y(x, high, from_x, from_high) for from_x in range(4) for from_high in range(2)]
+def column_places():
+    x, high = lax.axis_index("x"), lax.axis_index("high")
+    return [
+        [
+            (2 * half + core) * SIDES["y"] + place_along_y(x, high, from_x, other)
+            for core in range(2)
+            for from_x in range(4)
+            for other in range(2)
+        ]
+        for half in range(2)
+    ]
+
+
+def row_places():
+    high = lax.axis_index("high")
+    return [
+        (core * 4 + to_x) * 2 + (1 - high if other else high)
+        for core in range(2)
+        for to_x in range(4)
+        for other in range(2)
+    ]
 
 
 def split(x):
@@ -119,7 +141,7 @@
     )
 
 
-def left_kernel(total, groups, gathered_ref, block_ref, outer_ref, out_ref):
+def left_kernel(total, places, gathered_ref, block_ref, outer_ref, out_ref):
     steps = 4
     pieces = gathered_ref.shape[0] // total
     b_high, b_low = split(load_rows(gathered_ref, 0, total, pieces))
@@ -132,8 +154,8 @@
         mine = jnp.concatenate([mine] * (total // seqs), axis=0)
         for h in range(2):
             out_ref[pl.ds(h * total * turn + p, total, stride=turn), :] = mine
-    places = groups()
-    tall = total // len(places)
+    places = places()
+    block = seqs * turn
     rows = outer_ref.shape[0] // 2
     span = rows // steps
     for n in range(steps):
@@ -143,25 +165,22 @@
         left = left * (1.0 / total)
         for m in range(span // LANES):
             h, p = divmod(n * (span // LANES) + m, pieces)
-            for g, place in enumerate(places):
-                row = pl.multiple_of(place * (2 * tall * turn), 2 * tall * turn) + h * tall * turn + pieces + p
-                out_ref[pl.ds(row, tall, stride=turn), :] = left[
-                    g * tall : (g + 1) * tall, m * LANES : (m + 1) * LANES
+            for k, place in enumerate(places[h]):
+                row = pl.multiple_of(place * block, block) + pieces + p
+                out_ref[pl.ds(row, seqs, stride=turn), :] = left[
+                    k * seqs : (k + 1) * seqs, m * LANES : (m + 1) * LANES
                 ]
 
 
-def right_kernel(total, seqs, groups, gathered_ref, outer_ref, out_ref, sum_ref):
+def right_kernel(total, seqs, places, row_places, gathered_ref, outer_ref, out_ref, sum_ref):
     turn = gathered_ref.shape[0] // (2 * total)
     pieces = turn // 2
-    places = groups()
-    tall = total // len(places)
+    places = places()
+    block = seqs * turn
 
     def load(h, p):
-        rows = [
-            pl.multiple_of(place * (2 * tall * turn), 2 * tall * turn) + h * tall * turn + p
-            for place in places
-        ]
-        return jnp.concatenate([gathered_ref[pl.ds(r, tall, stride=turn), :] for r in rows], axis=0)
+        rows = [pl.multiple_of(place * block, block) + p for place in places[h]]
+        return jnp.concatenate([gathered_ref[pl.ds(r, seqs, stride=turn), :] for r in rows], axis=0)
 
     a_full = jnp.concatenate([load(h, p) for h in range(2) for p in range(pieces)], axis=1)
     a_high, a_low = split(a_full)
@@ -169,15 +188,19 @@
     both = product(jnp.concatenate([a_high, a_low], axis=0), outer_ref[:rows, :], NN)
     right = both[:total] + both[total:] + product(a_high, outer_ref[rows:, :], NN)
     right = right * (1.0 / total)
-    block = seqs * turn
     chunks = [gathered_ref[k : k + block, :] for k in range(0, gathered_ref.shape[0], block)]
     while len(chunks) > 1:
         chunks = [a + b for a, b in zip(chunks[::2], chunks[1::2])]
     for s in range(seqs):
         sum_ref[s * pieces : (s + 1) * pieces, :] = chunks[0][s * turn + pieces : (s + 1) * turn]
     pieces = out_ref.shape[0] // total
-    for p in range(pieces):
-        out_ref[pl.ds(p, total, stride=pieces), :] = right[:, p * LANES : (p + 1) * LANES]
+    block = seqs * pieces
+    for k, place in enumerate(row_places()):
+        for p in range(pieces):
+            row = pl.multiple_of(place * block, block) + p
+            out_ref[pl.ds(row, seqs, stride=pieces), :] = right[
+                k * seqs : (k + 1) * seqs, p * LANES : (p + 1) * LANES
+            ]
 
 
 def pack_kernel(feat_c, feat_e, left_ref, right_ref, block_ref, spread_ref, flat_ref):
@@ -246,17 +269,17 @@
     )[0]
 
 
-def local_left(total, gathered, block, outer, rows, groups=groups_along_y, **how):
+def local_left(total, gathered, block, outer, rows, places=column_places, **how):
     return call(
-        functools.partial(left_kernel, total, groups), [(((rows, LANES), jnp.float32), True)],
+        functools.partial(left_kernel, total, places), [(((rows, LANES), jnp.float32), True)],
         [(gathered, True), (block, True), (outer, True)], **how,
     )[0]
 
 
-def local_right(total, seqs, gathered, outer, rows, block_rows, groups=groups_along_y, **how):
+def local_right(total, seqs, gathered, outer, rows, block_rows, places=column_places, row_places=row_places, **how):
     f32 = jnp.float32
     return call(
-        functools.partial(right_kernel, total, seqs, groups),
+        functools.partial(right_kernel, total, seqs, places, row_places),
         [(((rows, LANES), f32), True), (((block_rows, LANES), f32), True)],
         [(gathered, True), (outer, True)], **how,
     )
@@ -294,31 +317,34 @@
 
 
 def compute(left, right, grad, mapping):
-    rows, cols = lax.axis_size("row"), lax.axis_size("col")
+    rows, cols = lax.axis_size(ROW), lax.axis_size(COL)
     seqs, _, feat_c = left.shape
     feat_e = right.shape[2]
     total = seqs * rows
     moves = pair_moves()
     back = [(b, a) for a, b in moves]
-    both = ("row", "col")
-
-    left_block, right_spread = pack(left, right, rows)
+
+    left_block, right_block = pack(left, right, 1)
     block_rows = left_block.shape[0]
-    left_block = lax.ppermute(left_block, both, moves)
-    right_all = to_each(right_spread, "row").reshape(-1, LANES)
+    across = lax.ppermute(right_block, "high", [(0, 1), (1, 0)])
+    left_block = lax.ppermute(left_block, ALL, moves)
+    near = lax.axis_size(NEAR)
+    spread = jnp.broadcast_to(jnp.concatenate([right_block, across])[None], (near, 2 * block_rows, LANES))
+    right_all = to_each(spread, NEAR).reshape(-1, LANES)
     outer = local_outer(grad, mapping, feat_c, feat_e)
     shared = local_left(total, right_all, left_block, outer, cols * 2 * block_rows)
-    shared = to_each(shared, "col").reshape(-1, LANES)
+    shared = to_each(shared, COL).reshape(-1, LANES)
     right_part, left_sum = local_right(
-        total, seqs, shared, outer, right_spread.shape[0], block_rows
-    )
-    left_sum = lax.ppermute(left_sum, both, back)
-    right_parts = to_each(right_part, "row").reshape(-1, LANES)
+        total, seqs, shared, outer, rows * block_rows, block_rows
+    )
+    left_sum = lax.ppermute(left_sum, ALL, back)
+    right_parts = to_each(right_part, ROW).reshape(-1, LANES)
     return unpack(left_sum, right_parts, left, right)
 
 
 def solution(mesh):
-    spec = P("row", "col", None)
+    mesh = Mesh(mesh.devices.reshape(tuple(SIDES.values())), ALL)
+    spec = P(ALL[:3], ALL[3:], None)
     return jax.shard_map(
         compute,
         mesh=mesh,

time: 78.6 us -> 83.6 us (1.064)
  starting transfers between devices: 33.7 us -> 36.3 us
  waiting for transfers between devices: 9.92 us -> 11.9 us
    ppermute x2 -> x3, starting transfers between devices: 10.5 us -> 21 us  [the longest x1 10.9 us: compute(): across = lax.ppermute(right_block, 'high', [(0, 1), (1, 0)])]
    all_to_all x2, starting transfers between devices: 23.2 us -> 15.3 us  [to_each(): return lax.all_to_all(chunks, axis, split_axis=0, concat_axis=0, tiled=True)]
    ppermute x2 -> x3, waiting for transfers between devices: 9.92 us -> 11.9 us  [the longest x1 9.45 us: compute(): left_sum = lax.ppermute(left_sum, ALL, back)]
  transfers between devices with their start and end apart: 4 -> 5, of which waited for: 2 -> 3; matrix products, arithmetic and copies ran while one was open for 0% -> 0% of each run, Pallas kernels for 3% -> 3%
where the time goes in v6:
time: 83.6 us; the launch traced here: 83.1 us
  starting transfers between devices  36.3 us (43%)
  blocking collectives  27.2 us (33%)
  waiting for transfers between devices  11.9 us (14%)
  Pallas kernels  6.38 us (8%)
    all_to_all x1, blocking collectives, to_each(): return lax.all_to_all(chunks, axis, split_axis=0, concat_axis=0, tiled=True)  27.2 us
    all_to_all x2, starting transfers between devices, to_each(): return lax.all_to_all(chunks, axis, split_axis=0, concat_axis=0, tiled=True)  15.3 us
    ppermute x1, starting transfers between devices, compute(): across = lax.ppermute(right_block, 'high', [(0, 1), (1, 0)])  10.9 us
    ppermute x1, waiting for transfers between devices, compute(): left_sum = lax.ppermute(left_sum, ALL, back)  9.45 us
    ppermute x1, starting transfers between devices, compute(): left_block = lax.ppermute(left_block, ALL, moves)  7.14 us
    pallas_call x5, Pallas kernels, call(): pl.pallas_call(kernel, out_shape=tuple((kind(near)(shape, dtype) for (sha...  6.38 us
    ppermute x1, starting transfers between devices, compute(): left_sum = lax.ppermute(left_sum, ALL, back)  2.99 us
  transfers between devices with their start and end apart: 5, of which 3 were waited for; matrix products, arithmetic and copies ran while one was open for 0% of the time, Pallas kernels for 3%

profile of v6, /device:TPU:14, one launch (start us, length us, event | category | flops | bytes accessed | tf_op | source)
XLA Modules:
  0.0 83.1 jit_solution(10175005701597327270)
XLA Ops:
  0.6 0.9 %shard_map.59 = (f32[16,128]{1,0:T(8,128)S(1)}, f32[16,128]{1,0:T(8,128)S(1)}) custom-call(f32[64,32]{1,0:T(8,128)} %bitcast.15, f32[64,32]{1,0:T(8,128)} %bitcast.16), custom_call_target="tpu_custom_call" | custom-call | tf_op jit(solution)/shard_map/pallas_call | solution.py:246
  1.6 10.9 %collective-permute-start = (f32[16,128]{1,0:T(8,128)S(1)}, f32[16,128]{1,0:T(8,128)S(1)}, u32[]{:S(2)}, u32[]{:S(2)}) collective-permute-start(f32[16,128]{1,0:T(8,128)S(1)} %get-tuple-element.8), channel_id=1, source_target_pairs={{0,64},{64,0},{1,65},{65,1},{2,66},{66,2},{3,67},{67,3},{4,68},{68... | collective-permute-start | bytes 24584 | tf_op jit(solution)/shard_map/ppermute | solution.py:329
  12.5 1.6 %collective-permute-done = f32[16,128]{1,0:T(8,128)S(1)} collective-permute-done((f32[16,128]{1,0:T(8,128)S(1)}, f32[16,128]{1,0:T(8,128)S(1)}, u32[]{:S(2)}, u32[]{:S(2)}) %collective-permute-start) | collective-permute-done | bytes 8224 | tf_op jit(solution)/shard_map/ppermute | solution.py:329
  14.1 0.7 broadcast_in_dim.2
  14.8 4.8 %all-to-all-start = ((f32[8,32,128]{2,1,0:T(8,128)}), f32[8,32,128]{2,1,0:T(8,128)S(1)}, u32[]{:S(2)}, u32[]{:S(2)}) async-start(f32[8,32,128]{2,1,0:T(8,128)} %broadcast_in_dim.2), calls=%async_computation | async-start | bytes 262144 | tf_op jit(solution)/shard_map/all_to_all | solution.py:316
  19.6 7.1 %collective-permute-start.1 = (f32[16,128]{1,0:T(8,128)S(1)}, f32[16,128]{1,0:T(8,128)S(1)}, u32[]{:S(2)}, u32[]{:S(2)}) collective-permute-start(f32[16,128]{1,0:T(8,128)S(1)} %get-tuple-element.9), channel_id=1, source_target_pairs={{0,16},{1,18},{2,48},{3,50},{4,76},{5,78},{6,108},{7,110},{8,156},... | collective-permute-start | bytes 24584 | tf_op jit(solution)/shard_map/ppermute | solution.py:330
  26.7 2.7 %shard_map.60.outer_ref = bf16[2048,512]{1,0:T(8,128)(2,1)S(1)} custom-call(f32[512,128]{1,0:T(8,128)} %bitcast.14, f32[1024,128]{1,0:T(8,128)} %map_hbm.1), custom_call_target="tpu_custom_call" | custom-call | tf_op jit(solution)/shard_map/pallas_call | solution.py:246
  29.4 0.8 collective-permute-done.1.block_ref
  30.2 0.0 all-to-all-done
  30.2 0.8 %shard_map.61 = f32[1024,128]{1,0:T(8,128)S(1)} custom-call(f32[256,128]{1,0:T(8,128)S(1)} %bitcast.13, f32[16,128]{1,0:T(8,128)S(1)} %collective-permute-done.1.block_ref, bf16[2048,512]{1,0:T(8,128)(2,1)S(1)} %shard_map.60.outer_ref), custom_call_target="tpu_custom_call" | custom-call | tf_op jit(solution)/shard_map/pallas_call | solution.py:246
  31.1 27.2 %all_to_all.15 = f32[32,32,128]{2,1,0:T(8,128)S(1)} all-to-all(f32[32,32,128]{2,1,0:T(8,128)S(1)} %bitcast.11), channel_id=1, replica_groups=mesh['x'=4,'high'=2,'core'=2,'y'=8,'low'=4] {'low','y'}, dimensions={0} | all-to-all | bytes 1048576 | tf_op jit(solution)/shard_map/all_to_all | solution.py:316
  58.3 1.1 %shard_map.62 = (f32[256,128]{1,0:T(8,128)}, f32[16,128]{1,0:T(8,128)S(1)}) custom-call(f32[1024,128]{1,0:T(8,128)S(1)} %bitcast.10, bf16[2048,512]{1,0:T(8,128)(2,1)S(1)} %shard_map.60.outer_ref), custom_call_target="tpu_custom_call" | custom-call | tf_op jit(solution)/shard_map/pallas_call | solution.py:246
  59.4 10.5 %all-to-all-start.2 = ((f32[16,16,128]{2,1,0:T(8,128)}), f32[16,16,128]{2,1,0:T(8,128)S(1)}, u32[]{:S(2)}, u32[]{:S(2)}) async-start(f32[16,16,128]{2,1,0:T(8,128)} %bitcast.6), calls=%async_computation.2 | async-start | bytes 262144 | tf_op jit(solution)/shard_map/all_to_all | solution.py:316
  69.9 3.0 %collective-permute-start.2 = (f32[16,128]{1,0:T(8,128)S(1)}, f32[16,128]{1,0:T(8,128)S(1)}, u32[]{:S(2)}, u32[]{:S(2)}) collective-permute-start(f32[16,128]{1,0:T(8,128)S(1)} %get-tuple-element.10), channel_id=1, source_target_pairs={{16,0},{18,1},{48,2},{50,3},{76,4},{78,5},{108,6},{110,7},{156,8},... | collective-permute-start | bytes 24584 | tf_op jit(solution)/shard_map/ppermute | solution.py:340
  72.9 9.5 %collective-permute-done.2.sum_ref = f32[16,128]{1,0:T(8,128)S(1)} collective-permute-done((f32[16,128]{1,0:T(8,128)S(1)}, f32[16,128]{1,0:T(8,128)S(1)}, u32[]{:S(2)}, u32[]{:S(2)}) %collective-permute-start.2) | collective-permute-done | bytes 8224 | tf_op jit(solution)/shard_map/ppermute | solution.py:340
  82.4 0.0 all-to-all-done.2
  82.4 0.8 shard_map.63
  (1 shorter events, 0.0 us)
Async XLA Ops:
  1.6 12.5 %collective-permute-start = (f32[16,128]{1,0:T(8,128)S(1)}, f32[16,128]{1,0:T(8,128)S(1)}, u32[]{:S(2)}, u32[]{:S(2)}) collective-permute-start(f32[16,128]{1,0:T(8,128)S(1)} %get-tuple-element.8), channel_id=1, source_target_pairs={{0,64},{64,0},{1,65},{65,1},{2,66},{66,2},{3,67},{67,3},{4,68},{68... | collective-permute-start | bytes 24584 | tf_op jit(solution)/shard_map/ppermute | solution.py:329
  14.8 15.4 %all-to-all-start = ((f32[8,32,128]{2,1,0:T(8,128)}), f32[8,32,128]{2,1,0:T(8,128)S(1)}, u32[]{:S(2)}, u32[]{:S(2)}) async-start(f32[8,32,128]{2,1,0:T(8,128)} %broadcast_in_dim.2), calls=%async_computation | async-start | bytes 262144 | tf_op jit(solution)/shard_map/all_to_all | solution.py:316
  19.6 10.7 %collective-permute-start.1 = (f32[16,128]{1,0:T(8,128)S(1)}, f32[16,128]{1,0:T(8,128)S(1)}, u32[]{:S(2)}, u32[]{:S(2)}) collective-permute-start(f32[16,128]{1,0:T(8,128)S(1)} %get-tuple-element.9), channel_id=1, source_target_pairs={{0,16},{1,18},{2,48},{3,50},{4,76},{5,78},{6,108},{7,110},{8,156},... | collective-permute-start | bytes 24584 | tf_op jit(solution)/shard_map/ppermute | solution.py:330
  59.4 23.0 %all-to-all-start.2 = ((f32[16,16,128]{2,1,0:T(8,128)}), f32[16,16,128]{2,1,0:T(8,128)S(1)}, u32[]{:S(2)}, u32[]{:S(2)}) async-start(f32[16,16,128]{2,1,0:T(8,128)} %bitcast.6), calls=%async_computation.2 | async-start | bytes 262144 | tf_op jit(solution)/shard_map/all_to_all | solution.py:316
  69.9 12.4 %collective-permute-start.2 = (f32[16,128]{1,0:T(8,128)S(1)}, f32[16,128]{1,0:T(8,128)S(1)}, u32[]{:S(2)}, u32[]{:S(2)}) collective-permute-start(f32[16,128]{1,0:T(8,128)S(1)} %get-tuple-element.10), channel_id=1, source_target_pairs={{16,0},{18,1},{48,2},{50,3},{76,4},{78,5},{108,6},{110,7},{156,8},... | collective-permute-start | bytes 24584 | tf_op jit(solution)/shard_map/ppermute | solution.py:340

commit v7 on v6

--- a/solution.py
+++ b/solution.py
@@ -218,7 +218,7 @@
     block_ref[...] = jnp.concatenate(pieces, axis=1)
 
 
-def unpack_kernel(feat_c, feat_e, sum_ref, parts_ref, left_ref, right_ref, flat_ref):
+def unpack_left_kernel(feat_c, sum_ref, left_ref, flat_ref):
     count = sum_ref.shape[0]
     res = LANES * count // flat_ref.shape[0]
     group = LANES // res
@@ -226,6 +226,10 @@
         flat_ref[pl.ds(g, count, stride=group), :] = sum_ref[:, g * res : (g + 1) * res]
     for s in range(left_ref.shape[0] // res):
         left_ref[s * res : (s + 1) * res, :] = flat_ref[s * feat_c : (s + 1) * feat_c, :].T
+
+
+def unpack_right_kernel(feat_e, parts_ref, right_ref):
+    count = right_ref.shape[0] * feat_e // LANES
     parts = [parts_ref[k : k + count, :] for k in range(0, parts_ref.shape[0], count)]
     while len(parts) > 1:
         parts = [a + b for a, b in zip(parts[::2], parts[1::2])]
@@ -298,17 +302,23 @@
     )
 
 
-def unpack(left_sum, right_parts, left, right, **how):
+def unpack_left(left_sum, left, **how):
     seqs, res, feat_c = left.shape
-    feat_e = right.shape[2]
-    f32 = jnp.float32
-    outs = call(
-        functools.partial(unpack_kernel, feat_c, feat_e),
-        [(((seqs * res, feat_c), f32), None), (((seqs * res, feat_e), f32), None)],
-        [(left_sum, True), (right_parts, True)],
-        [pltpu.VMEM((seqs * feat_c, res), f32)], **how,
-    )
-    return outs[0].reshape(left.shape), outs[1].reshape(right.shape)
+    out = call(
+        functools.partial(unpack_left_kernel, feat_c),
+        [(((seqs * res, feat_c), jnp.float32), None)], [(left_sum, True)],
+        [pltpu.VMEM((seqs * feat_c, res), jnp.float32)], **how,
+    )[0]
+    return out.reshape(left.shape)
+
+
+def unpack_right(right_parts, right, **how):
+    seqs, res, feat_e = right.shape
+    out = call(
+        functools.partial(unpack_right_kernel, feat_e),
+        [(((seqs * res, feat_e), jnp.float32), None)], [(right_parts, True)], **how,
+    )[0]
+    return out.reshape(right.shape)
 
 
 def to_each(chunks, axis):
@@ -339,7 +349,8 @@
     )
     left_sum = lax.ppermute(left_sum, ALL, back)
     right_parts = to_each(right_part, ROW).reshape(-1, LANES)
-    return unpack(left_sum, right_parts, left, right)
+    grad_right = unpack_right(right_parts, right)
+    return unpack_left(left_sum, left), grad_right
 
 
 def solution(mesh):

time: 83.6 us -> 84.3 us (level)
    pallas_call x5 -> x6, Pallas kernels: 6.38 us -> 7.06 us  [call(): pl.pallas_call(kernel, out_shape=tuple((kind(near)(shape, dtype) for (sha...]
  transfers between devices with their start and end apart: 5 -> 5, of which waited for: 3 -> 3; matrix products, arithmetic and copies ran while one was open for 0% -> 0% of each run, Pallas kernels for 3% -> 4%
where the time goes in v7:
time: 84.3 us; the launch traced here: 83.8 us
  starting transfers between devices  36.3 us (43%)
  blocking collectives  27.2 us (32%)
  waiting for transfers between devices  11.9 us (14%)
  Pallas kernels  7.06 us (8%)
    all_to_all x1, blocking collectives, to_each(): return lax.all_to_all(chunks, axis, split_axis=0, concat_axis=0, tiled=True)  27.2 us
    all_to_all x2, starting transfers between devices, to_each(): return lax.all_to_all(chunks, axis, split_axis=0, concat_axis=0, tiled=True)  15.3 us
    ppermute x1, starting transfers between devices, compute(): across = lax.ppermute(right_block, 'high', [(0, 1), (1, 0)])  10.9 us
    ppermute x1, waiting for transfers between devices, compute(): left_sum = lax.ppermute(left_sum, ALL, back)  9.45 us
    ppermute x1, starting transfers between devices, compute(): left_block = lax.ppermute(left_block, ALL, moves)  7.14 us
    pallas_call x6, Pallas kernels, call(): pl.pallas_call(kernel, out_shape=tuple((kind(near)(shape, dtype) for (sha...  7.06 us
    ppermute x1, starting transfers between devices, compute(): left_sum = lax.ppermute(left_sum, ALL, back)  2.99 us
  transfers between devices with their start and end apart: 5, of which 3 were waited for; matrix products, arithmetic and copies ran while one was open for 0% of the time, Pallas kernels for 4%

profile of v7, /device:TPU:14, one launch (start us, length us, event | category | flops | bytes accessed | tf_op | source)
XLA Modules:
  0.0 83.8 jit_solution(6388524614703802944)
XLA Ops:
  0.6 0.9 %shard_map.59 = (f32[16,128]{1,0:T(8,128)S(1)}, f32[16,128]{1,0:T(8,128)S(1)}) custom-call(f32[64,32]{1,0:T(8,128)} %bitcast.17, f32[64,32]{1,0:T(8,128)} %bitcast.18), custom_call_target="tpu_custom_call" | custom-call | tf_op jit(solution)/shard_map/pallas_call | solution.py:250
  1.6 10.9 %collective-permute-start = (f32[16,128]{1,0:T(8,128)S(1)}, f32[16,128]{1,0:T(8,128)S(1)}, u32[]{:S(2)}, u32[]{:S(2)}) collective-permute-start(f32[16,128]{1,0:T(8,128)S(1)} %get-tuple-element.6), channel_id=1, source_target_pairs={{0,64},{64,0},{1,65},{65,1},{2,66},{66,2},{3,67},{67,3},{4,68},{68... | collective-permute-start | bytes 24584 | tf_op jit(solution)/shard_map/ppermute | solution.py:339
  12.5 1.6 %collective-permute-done = f32[16,128]{1,0:T(8,128)S(1)} collective-permute-done((f32[16,128]{1,0:T(8,128)S(1)}, f32[16,128]{1,0:T(8,128)S(1)}, u32[]{:S(2)}, u32[]{:S(2)}) %collective-permute-start) | collective-permute-done | bytes 8224 | tf_op jit(solution)/shard_map/ppermute | solution.py:339
  14.1 0.7 broadcast_in_dim.2
  14.8 4.8 %all-to-all-start = ((f32[8,32,128]{2,1,0:T(8,128)}), f32[8,32,128]{2,1,0:T(8,128)S(1)}, u32[]{:S(2)}, u32[]{:S(2)}) async-start(f32[8,32,128]{2,1,0:T(8,128)} %broadcast_in_dim.2), calls=%async_computation | async-start | bytes 262144 | tf_op jit(solution)/shard_map/all_to_all | solution.py:326
  19.6 7.1 %collective-permute-start.1 = (f32[16,128]{1,0:T(8,128)S(1)}, f32[16,128]{1,0:T(8,128)S(1)}, u32[]{:S(2)}, u32[]{:S(2)}) collective-permute-start(f32[16,128]{1,0:T(8,128)S(1)} %get-tuple-element.7), channel_id=1, source_target_pairs={{0,16},{1,18},{2,48},{3,50},{4,76},{5,78},{6,108},{7,110},{8,156},... | collective-permute-start | bytes 24584 | tf_op jit(solution)/shard_map/ppermute | solution.py:340
  26.7 2.7 %shard_map.60.outer_ref = bf16[2048,512]{1,0:T(8,128)(2,1)S(1)} custom-call(f32[512,128]{1,0:T(8,128)} %bitcast.14, f32[1024,128]{1,0:T(8,128)} %map_hbm.1), custom_call_target="tpu_custom_call" | custom-call | tf_op jit(solution)/shard_map/pallas_call | solution.py:250
  29.4 0.8 collective-permute-done.1.block_ref
  30.2 0.0 all-to-all-done
  30.2 0.8 shard_map.61
  31.1 27.2 %all_to_all.15 = f32[32,32,128]{2,1,0:T(8,128)S(1)} all-to-all(f32[32,32,128]{2,1,0:T(8,128)S(1)} %bitcast.11), channel_id=1, replica_groups=mesh['x'=4,'high'=2,'core'=2,'y'=8,'low'=4] {'low','y'}, dimensions={0} | all-to-all | bytes 1048576 | tf_op jit(solution)/shard_map/all_to_all | solution.py:326
  58.3 1.1 %shard_map.62 = (f32[256,128]{1,0:T(8,128)}, f32[16,128]{1,0:T(8,128)S(1)}) custom-call(f32[1024,128]{1,0:T(8,128)S(1)} %bitcast.10, bf16[2048,512]{1,0:T(8,128)(2,1)S(1)} %shard_map.60.outer_ref), custom_call_target="tpu_custom_call" | custom-call | tf_op jit(solution)/shard_map/pallas_call | solution.py:250
  59.4 10.5 %all-to-all-start.2 = ((f32[16,16,128]{2,1,0:T(8,128)}), f32[16,16,128]{2,1,0:T(8,128)S(1)}, u32[]{:S(2)}, u32[]{:S(2)}) async-start(f32[16,16,128]{2,1,0:T(8,128)} %bitcast.7), calls=%async_computation.2 | async-start | bytes 262144 | tf_op jit(solution)/shard_map/all_to_all | solution.py:326
  69.9 3.0 %collective-permute-start.2 = (f32[16,128]{1,0:T(8,128)S(1)}, f32[16,128]{1,0:T(8,128)S(1)}, u32[]{:S(2)}, u32[]{:S(2)}) collective-permute-start(f32[16,128]{1,0:T(8,128)S(1)} %get-tuple-element.8), channel_id=1, source_target_pairs={{16,0},{18,1},{48,2},{50,3},{76,4},{78,5},{108,6},{110,7},{156,8},... | collective-permute-start | bytes 24584 | tf_op jit(solution)/shard_map/ppermute | solution.py:350
  72.9 9.5 %collective-permute-done.2.sum_ref = f32[16,128]{1,0:T(8,128)S(1)} collective-permute-done((f32[16,128]{1,0:T(8,128)S(1)}, f32[16,128]{1,0:T(8,128)S(1)}, u32[]{:S(2)}, u32[]{:S(2)}) %collective-permute-start.2) | collective-permute-done | bytes 8224 | tf_op jit(solution)/shard_map/ppermute | solution.py:350
  82.3 0.8 shard_map.63
  83.1 0.0 all-to-all-done.2
  83.1 0.7 shard_map.64
  (1 shorter events, 0.0 us)
Async XLA Ops:
  1.6 12.5 %collective-permute-start = (f32[16,128]{1,0:T(8,128)S(1)}, f32[16,128]{1,0:T(8,128)S(1)}, u32[]{:S(2)}, u32[]{:S(2)}) collective-permute-start(f32[16,128]{1,0:T(8,128)S(1)} %get-tuple-element.6), channel_id=1, source_target_pairs={{0,64},{64,0},{1,65},{65,1},{2,66},{66,2},{3,67},{67,3},{4,68},{68... | collective-permute-start | bytes 24584 | tf_op jit(solution)/shard_map/ppermute | solution.py:339
  14.8 15.4 %all-to-all-start = ((f32[8,32,128]{2,1,0:T(8,128)}), f32[8,32,128]{2,1,0:T(8,128)S(1)}, u32[]{:S(2)}, u32[]{:S(2)}) async-start(f32[8,32,128]{2,1,0:T(8,128)} %broadcast_in_dim.2), calls=%async_computation | async-start | bytes 262144 | tf_op jit(solution)/shard_map/all_to_all | solution.py:326
  19.6 10.7 %collective-permute-start.1 = (f32[16,128]{1,0:T(8,128)S(1)}, f32[16,128]{1,0:T(8,128)S(1)}, u32[]{:S(2)}, u32[]{:S(2)}) collective-permute-start(f32[16,128]{1,0:T(8,128)S(1)} %get-tuple-element.7), channel_id=1, source_target_pairs={{0,16},{1,18},{2,48},{3,50},{4,76},{5,78},{6,108},{7,110},{8,156},... | collective-permute-start | bytes 24584 | tf_op jit(solution)/shard_map/ppermute | solution.py:340
  59.4 23.7 %all-to-all-start.2 = ((f32[16,16,128]{2,1,0:T(8,128)}), f32[16,16,128]{2,1,0:T(8,128)S(1)}, u32[]{:S(2)}, u32[]{:S(2)}) async-start(f32[16,16,128]{2,1,0:T(8,128)} %bitcast.7), calls=%async_computation.2 | async-start | bytes 262144 | tf_op jit(solution)/shard_map/all_to_all | solution.py:326
  69.9 12.4 %collective-permute-start.2 = (f32[16,128]{1,0:T(8,128)S(1)}, f32[16,128]{1,0:T(8,128)S(1)}, u32[]{:S(2)}, u32[]{:S(2)}) collective-permute-start(f32[16,128]{1,0:T(8,128)S(1)} %get-tuple-element.8), channel_id=1, source_target_pairs={{16,0},{18,1},{48,2},{50,3},{76,4},{78,5},{108,6},{110,7},{156,8},... | collective-permute-start | bytes 24584 | tf_op jit(solution)/shard_map/ppermute | solution.py:350
